TPU v7x, 32 devices: a whole 2x2x4 slice. The times are simulated.
32 devices in a mesh: ens: 2 (over x), band: 16 (over z, y, core).
Axes of the slice: x: 2, y: 2, z: 4, core: 2. Of those that a mesh axis runs over, the one named last changes fastest.
Arguments:
- atm_state: bfloat16 [256, 128, 384], P(('ens', 'band')), parts along dimension 0, may hold values from -6 to 6
- ocean_state: bfloat16 [256, 128, 384], P(('ens', 'band')), parts along dimension 0, may hold values from -6 to 6
- dw_kernel: float32 [2, 7, 7, 384], replicated, may hold values from -0.875 to 0.875
- norm_gain: float32 [2, 384], replicated, may hold values from 0.1 to 1.9
- w_up: bfloat16 [2, 384, 1536], replicated, may hold values from -0.3125 to 0.3125
- b_up: float32 [2, 1536], replicated, may hold values from -3 to 3
- w_down: bfloat16 [2, 384, 1536], replicated, may hold values from -0.15625 to 0.15625
- flux_out: bfloat16 [384, 256], replicated, may hold values from -0.3125 to 0.3125
- flux_in: bfloat16 [256, 384], replicated, may hold values from -0.375 to 0.375
- partner: int32 [32], P('ens'), parts along dimension 0, may hold values from 0 to 15, each once
- remap: int32 [256], P('ens'), parts along dimension 0, may hold values from 0 to 7
- land_mask: int32 [256, 128], P(('ens', 'band')), parts along dimension 0, may hold values 0 or 1
Outputs:
- atm_next: bfloat16 [256, 128, 384], P(('ens', 'band')), parts along dimension 0
- ocean_next: bfloat16 [256, 128, 384], P(('ens', 'band')), parts along dimension 0
There are 2 independent parts, one for each index of `ens`. A program takes and returns all parts, laid end to end along the dimension named above; an argument that names none is the same for every part. Nothing has to cross between parts.
Inputs may be any that keep to these rules, and one draw needn't show every extreme that they name: Each of the 16 atmosphere bands is the partner of exactly one ocean band.
All inputs are finite; a program needn't handle non-finite values. No bound on the sum of `land_mask` on one device may be relied on, other than what follows from the above.
Results may differ from a plain program's by a relative error of at most 0.0075.
Values may be sent and summed in bfloat16 or wider, within the bound.
No kernel may reach another device: no remote copies, remote signals or barrier semaphores. Data moves between devices by JAX's collectives and lax.ppermute only.
A program may use at most 64 MiB of HBM per device.

v0:
```python
import jax
import jax.numpy as jnp
from jax import lax
from jax.sharding import PartitionSpec as P


def with_halo(array, sides, width):
    for axis, dim in sides:
        size, length = (lax.axis_size(axis), array.shape[dim])
        up = [(i, (i + 1) % size) for i in range(size - 1)]
        down = [(j, i) for i, j in up]
        last = lax.slice_in_dim(array, length - width, length, axis=dim)
        first = lax.slice_in_dim(array, 0, width, axis=dim)
        before = lax.ppermute(last, axis, up)
        after = lax.ppermute(first, axis, down)
        array = jnp.concatenate([before, array, after], axis=dim)
    return array


def conv_norm(field, kernel, gain):
    padded = with_halo(field, (("band", 0),), 3)
    padded = jnp.concatenate([padded[:, -3:], padded, padded[:, :3]], axis=1).astype(jnp.float32)
    height, width = (field.shape[0], field.shape[1])
    total = jnp.zeros(field.shape, jnp.float32)
    for a in range(7):
        for b in range(7):
            total = total + kernel[a, b] * padded[a : a + height, b : b + width]
    center = jnp.mean(total, axis=-1, keepdims=True)
    spread = jnp.mean((total - center) ** 2, axis=-1, keepdims=True)
    normed = ((total - center) * lax.rsqrt(spread + 1e-06) * gain).astype(jnp.bfloat16)
    return normed.reshape(height * width, field.shape[2])


def mixer(field, which, dw_kernel, norm_gain, w_up, b_up, w_down):
    normed = conv_norm(field, dw_kernel[which], norm_gain[which])
    hidden = jax.nn.gelu(
        jnp.dot(normed, w_up[which], preferred_element_type=jnp.float32) + b_up[which],
        approximate=True,
    ).astype(jnp.bfloat16)
    update = lax.dot_general(
        hidden, w_down[which], (((1,), (1,)), ((), ())), preferred_element_type=jnp.float32
    )
    return (field.astype(jnp.float32) + update.reshape(field.shape)).astype(jnp.bfloat16)


def partner_move(tile, indices):
    picked = jnp.take(
        lax.all_to_all(tile, "band", split_axis=1, concat_axis=0, tiled=True), indices, axis=0
    )
    return lax.all_to_all(picked, "band", split_axis=0, concat_axis=1, tiled=True)


def per_device(
    atm_state,
    ocean_state,
    dw_kernel,
    norm_gain,
    w_up,
    b_up,
    w_down,
    flux_out,
    flux_in,
    partner,
    remap,
    land_mask,
):
    atm_next = mixer(atm_state, 0, dw_kernel, norm_gain, w_up, b_up, w_down)
    height, width, channels = atm_next.shape
    band_rows = remap.shape[0] // partner.shape[0]
    indices = jnp.repeat(partner, band_rows) * band_rows + remap
    surface = jnp.dot(
        atm_next.reshape(-1, channels), flux_out, preferred_element_type=jnp.float32
    ).astype(jnp.bfloat16)
    moved = partner_move(surface.reshape(height, width, -1), indices).reshape(height * width, -1)
    forcing = jnp.dot(moved, flux_in, preferred_element_type=jnp.float32).reshape(
        height, width, channels
    )
    ocean_in = (
        ocean_state.astype(jnp.float32) + land_mask.astype(jnp.float32)[:, :, None] * forcing
    ).astype(jnp.bfloat16)
    ocean_next = mixer(ocean_in, 1, dw_kernel, norm_gain, w_up, b_up, w_down)
    return (atm_next, ocean_next)


def solution(mesh):
    in_specs = (
        P(("ens", "band"), None, None),
        P(("ens", "band"), None, None),
        P(),
        P(),
        P(),
        P(),
        P(),
        P(),
        P(),
        P("ens"),
        P("ens"),
        P(("ens", "band"), None),
    )
    out_specs = (P(("ens", "band"), None, None), P(("ens", "band"), None, None))
    return jax.shard_map(
        per_device, mesh=mesh, in_specs=in_specs, out_specs=out_specs, check_vma=False
    )
```

profile of v0, /device:TPU:9, one launch (start us, length us, event | category | flops | bytes accessed | tf_op | source)
XLA Modules:
  0.0 110.5 jit_solution(1870685209608916670)
XLA Ops:
  0.7 1.2 %fusion.132 = (bf16[3,128,384]{2,1,0:T(8,128)(2,1)S(1)}, bf16[3,128,384]{2,1,0:T(8,128)(2,1)S(1)}) fusion(bf16[8,128,384]{2,1,0:T(8,128)(2,1)} %param.12), kind=kLoop, calls=%fused_computation.360 | loop fusion | bytes 1179648 | tf_op jit(solution)/shard_map/slice | solution.py:13
  1.9 2.6 %collective-permute-start.1 = (bf16[3,128,384]{2,1,0:T(8,128)(2,1)S(1)}, bf16[3,128,384]{2,1,0:T(8,128)(2,1)S(1)}, u32[]{:S(2)}, u32[]{:S(2)}) collective-permute-start(bf16[3,128,384]{2,1,0:T(8,128)(2,1)S(1)} %get-tuple-element.114), channel_id=1, source_target_pairs={{1,0},{2,1},{3,2},{4,3},{5,4},{6,5},{7,6},{8,7},{9,8},{10,9},{11,1... | collective-permute-start | bytes 884744 | tf_op jit(solution)/shard_map/ppermute | solution.py:15
  4.5 3.0 %collective-permute-start = (bf16[3,128,384]{2,1,0:T(8,128)(2,1)S(1)}, bf16[3,128,384]{2,1,0:T(8,128)(2,1)S(1)}, u32[]{:S(2)}, u32[]{:S(2)}) collective-permute-start(bf16[3,128,384]{2,1,0:T(8,128)(2,1)S(1)} %get-tuple-element.115), channel_id=1, source_target_pairs={{0,1},{1,2},{2,3},{3,4},{4,5},{5,6},{6,7},{7,8},{8,9},{9,10},{10,1... | collective-permute-start | bytes 884744 | tf_op jit(solution)/shard_map/ppermute | solution.py:14
  7.5 1.1 %fusion.133 = (f32[1,7,7,384]{3,0,2,1:T(1,128)S(1)}, f32[1,7,7,384]{3,0,2,1:T(1,128)S(1)}) fusion(f32[2,7,7,384]{3,0,2,1:T(2,128)} %param.14), kind=kLoop, calls=%fused_computation.361 | loop fusion | bytes 301056 | tf_op jit(solution)/shard_map/slice | solution.py:35
  9.0 4.3 %collective-permute-done = bf16[3,128,384]{2,1,0:T(8,128)(2,1)S(1)} collective-permute-done((bf16[3,128,384]{2,1,0:T(8,128)(2,1)S(1)}, bf16[3,128,384]{2,1,0:T(8,128)(2,1)S(1)}, u32[]{:S(2)}, u32[]{:S(2)}) %collective-permute-start) | collective-permute-done | bytes 294944 | tf_op jit(solution)/shard_map/ppermute | solution.py:14
  14.0 12.0 %fusion.128 = (f32[8,128]{1,0:T(8,128)S(1)}, f32[8,128,384]{2,1,0:T(8,128)}) fusion(f32[14,134,384]{2,1,0:T(8,128)S(1)} %maximum_convert_fusion, f32[384]{0:T(512)S(1)} %get-tuple-element.52, f32[384]{0:T(512)S(1)} %get-tuple-element.53, f32[384]{0:T(512)S(1)} %get-tuple-element.54, f32[384]{0:T(512)S(1)} %get-tuple-element.55, ...), kind=kLoop, calls=%fused_computation.357 | loop fusion | flops 38534144 | bytes 78722560 | tf_op jit(solution)/shard_map/reduce_sum | solution.py:28
  25.9 1.9 %multiply_reduce_fusion.1 = f32[8,128]{1,0:T(8,128)S(1)} fusion(f32[8,128,384]{2,1,0:T(8,128)} %get-tuple-element.109, f32[8,128]{1,0:T(8,128)S(1)} %broadcast_multiply_fusion.1), kind=kLoop, calls=%fused_computation.219 | loop fusion | flops 1178624 | bytes 1581056 | tf_op jit(solution)/shard_map/reduce_sum | solution.py:29
  28.2 1.3 %copy-done.13 = bf16[2,384,1536]{2,1,0:T(8,128)(2,1)S(1)} copy-done((bf16[2,384,1536]{2,1,0:T(8,128)(2,1)S(1)}, bf16[2,384,1536]{2,1,0:T(8,128)(2,1)}, u32[]{:S(2)}) %copy-start.13) | copy-done | bytes 2359320
  29.5 2.9 %fusion.7 = bf16[1024,1536]{1,0:T(8,128)(2,1)S(1)} fusion(bf16[1024,384]{1,0:T(8,128)(2,1)S(1)} %bitcast.48, f32[1536]{0:T(1024)S(1)} %get-tuple-element.101, bf16[2,384,1536]{2,1,0:T(8,128)(2,1)S(1)} %copy-done.13), kind=kOutput, calls=%fused_computation.10 | convolution fusion | flops 1223688192 | bytes 5120000 | tf_op jit(solution)/shard_map/dot_general | solution.py:37
  32.4 1.8 %add_convert_fusion.2 = bf16[8,128,384]{2,1,0:T(8,128)(2,1)S(1)} fusion(bf16[8,128,384]{2,1,0:T(8,128)(2,1)S(1)} %copy-done.6, bf16[8,128,1536]{2,1,0:T(8,128)(2,1)S(1)} %bitcast.51, bf16[2,384,1536]{2,1,0:T(8,128)(2,1)S(1)} %copy-done.15), kind=kOutput, calls=%fused_computation.217 | convolution fusion | flops 1209139200 | bytes 5898240 | tf_op jit(solution)/shard_map/dot_general | solution.py:40
  35.6 1.1 copy.22
  36.7 6.2 %all-to-all-start = ((bf16[8,128,256]{2,0,1:T(8,128)(2,1)}), bf16[8,128,256]{2,0,1:T(8,128)(2,1)S(1)}, u32[]{:S(2)}, u32[]{:S(2)}) async-start(bf16[8,128,256]{2,0,1:T(8,128)(2,1)} %copy.22), calls=%async_computation | async-start | bytes 1048576 | tf_op jit(solution)/shard_map/all_to_all | solution.py:48
  43.1 13.9 %all-to-all-done = bf16[8,128,256]{2,0,1:T(8,128)(2,1)S(1)} async-done(((bf16[8,128,256]{2,0,1:T(8,128)(2,1)}), bf16[8,128,256]{2,0,1:T(8,128)(2,1)S(1)}, u32[]{:S(2)}, u32[]{:S(2)}) %all-to-all-start) | async-done | bytes 524320 | tf_op jit(solution)/shard_map/all_to_all | solution.py:48
  58.8 4.3 %all-to-all-start.1 = ((bf16[128,8,256]{2,1,0:T(8,128)(2,1)}), bf16[128,8,256]{2,1,0:T(8,128)(2,1)S(1)}, u32[]{:S(2)}, u32[]{:S(2)}) async-start(bf16[128,8,256]{2,1,0:T(8,128)(2,1)} %broadcast_select_fusion), calls=%async_computation.1 | async-start | bytes 1048576 | tf_op jit(solution)/shard_map/all_to_all | solution.py:50
  63.2 14.1 %all-to-all-done.1 = bf16[128,8,256]{2,1,0:T(8,128)(2,1)S(1)} async-done(((bf16[128,8,256]{2,1,0:T(8,128)(2,1)}), bf16[128,8,256]{2,1,0:T(8,128)(2,1)S(1)}, u32[]{:S(2)}, u32[]{:S(2)}) %all-to-all-start.1) | async-done | bytes 524320 | tf_op jit(solution)/shard_map/all_to_all | solution.py:50
  77.8 2.5 %collective-permute-start.2 = (bf16[3,128,384]{2,1,0:T(8,128)(2,1)S(1)}, bf16[3,128,384]{2,1,0:T(8,128)(2,1)S(1)}, u32[]{:S(2)}, u32[]{:S(2)}) collective-permute-start(bf16[3,128,384]{2,1,0:T(8,128)(2,1)S(1)} %get-tuple-element.112), channel_id=1, source_target_pairs={{0,1},{1,2},{2,3},{3,4},{4,5},{5,6},{6,7},{7,8},{8,9},{9,10},{10,1... | collective-permute-start | bytes 884744 | tf_op jit(solution)/shard_map/ppermute | solution.py:14
  80.4 2.1 %collective-permute-start.3 = (bf16[3,128,384]{2,1,0:T(8,128)(2,1)S(1)}, bf16[3,128,384]{2,1,0:T(8,128)(2,1)S(1)}, u32[]{:S(2)}, u32[]{:S(2)}) collective-permute-start(bf16[3,128,384]{2,1,0:T(8,128)(2,1)S(1)} %get-tuple-element.113), channel_id=1, source_target_pairs={{1,0},{2,1},{3,2},{4,3},{5,4},{6,5},{7,6},{8,7},{9,8},{10,9},{11,1... | collective-permute-start | bytes 884744 | tf_op jit(solution)/shard_map/ppermute | solution.py:15
  82.7 1.3 %collective-permute-done.2 = bf16[3,128,384]{2,1,0:T(8,128)(2,1)S(1)} collective-permute-done((bf16[3,128,384]{2,1,0:T(8,128)(2,1)S(1)}, bf16[3,128,384]{2,1,0:T(8,128)(2,1)S(1)}, u32[]{:S(2)}, u32[]{:S(2)}) %collective-permute-start.2) | collective-permute-done | bytes 294944 | tf_op jit(solution)/shard_map/ppermute | solution.py:14
  84.0 5.0 %collective-permute-done.3 = bf16[3,128,384]{2,1,0:T(8,128)(2,1)S(1)} collective-permute-done((bf16[3,128,384]{2,1,0:T(8,128)(2,1)S(1)}, bf16[3,128,384]{2,1,0:T(8,128)(2,1)S(1)}, u32[]{:S(2)}, u32[]{:S(2)}) %collective-permute-start.3) | collective-permute-done | bytes 294944 | tf_op jit(solution)/shard_map/ppermute | solution.py:15
  89.3 12.0 %fusion.126 = (f32[8,128]{1,0:T(8,128)S(1)}, f32[8,128,384]{2,1,0:T(8,128)}) fusion(f32[14,134,384]{2,1,0:T(8,128)S(1)} %fusion.113, f32[384]{0:T(512)S(1)} %get-tuple-element.3, f32[384]{0:T(512)S(1)} %get-tuple-element.4, f32[384]{0:T(512)S(1)} %get-tuple-element.5, f32[384]{0:T(512)S(1)} %get-tuple-element.6, f32[384]{0:T(512)S(1)} %get-tuple-element.7, ...), kind=kLoop, calls=%fused_computation.356 | loop fusion | flops 38534144 | bytes 78722560 | tf_op jit(solution)/shard_map/reduce_sum | solution.py:28
  101.3 1.9 %multiply_reduce_fusion = f32[8,128]{1,0:T(8,128)S(1)} fusion(f32[8,128,384]{2,1,0:T(8,128)} %get-tuple-element.105, f32[8,128]{1,0:T(8,128)S(1)} %broadcast_multiply_fusion), kind=kLoop, calls=%fused_computation.215 | loop fusion | flops 1178624 | bytes 1581056 | tf_op jit(solution)/shard_map/reduce_sum | solution.py:29
  103.6 1.3 %copy-done.14 = bf16[2,384,1536]{2,1,0:T(8,128)(2,1)S(1)} copy-done((bf16[2,384,1536]{2,1,0:T(8,128)(2,1)S(1)}, bf16[2,384,1536]{2,1,0:T(8,128)(2,1)}, u32[]{:S(2)}) %copy-start.14) | copy-done | bytes 2359320
  104.9 2.9 %fusion.15 = bf16[1024,1536]{1,0:T(8,128)(2,1)S(1)} fusion(bf16[1024,384]{1,0:T(8,128)(2,1)S(1)} %bitcast.47, f32[1536]{0:T(1024)S(1)} %get-tuple-element.100, bf16[2,384,1536]{2,1,0:T(8,128)(2,1)S(1)} %copy-done.14), kind=kOutput, calls=%fused_computation.18 | convolution fusion | flops 1223688192 | bytes 5120000 | tf_op jit(solution)/shard_map/dot_general | solution.py:37
  107.8 2.7 %add_convert_fusion = bf16[8,128,384]{2,1,0:T(8,128)(2,1)} fusion(bf16[8,128,384]{2,1,0:T(8,128)(2,1)S(1)} %copy-done.4, bf16[8,128,1536]{2,1,0:T(8,128)(2,1)S(1)} %bitcast.50, bf16[2,384,1536]{2,1,0:T(8,128)(2,1)S(1)} %copy-done.16), kind=kOutput, calls=%fused_computation.213 | convolution fusion | flops 1209139200 | bytes 5898240 | tf_op jit(solution)/shard_map/dot_general | solution.py:40
  (70 shorter events, 6.1 us)
Async XLA Ops:
  0.6 76.6 %copy-start = (bf16[256,384]{1,0:T(8,128)(2,1)S(1)}, bf16[256,384]{1,0:T(8,128)(2,1)}, u32[]{:S(2)}) copy-start(bf16[256,384]{1,0:T(8,128)(2,1)} %param.20) | copy-start | bytes 589828
  0.6 12.7 %copy-start.5 = (bf16[8,128,384]{2,1,0:T(8,128)(2,1)S(1)}, bf16[8,128,384]{2,1,0:T(8,128)(2,1)}, u32[]{:S(2)}) copy-start(bf16[8,128,384]{2,1,0:T(8,128)(2,1)} %param.12) | copy-start | bytes 2359300
  0.7 8.2 %copy-start.9 = (f32[2,1536]{1,0:T(2,128)S(1)}, f32[2,1536]{1,0:T(2,128)}, u32[]{:S(2)}) copy-start(f32[2,1536]{1,0:T(2,128)} %param.17) | copy-start | bytes 36868
  0.7 8.3 %copy-start.11 = (f32[2,384]{1,0:T(2,128)S(1)}, f32[2,384]{1,0:T(2,128)}, u32[]{:S(2)}) copy-start(f32[2,384]{1,0:T(2,128)} %param.15) | copy-start | bytes 9220
  1.9 11.6 %collective-permute-start.1 = (bf16[3,128,384]{2,1,0:T(8,128)(2,1)S(1)}, bf16[3,128,384]{2,1,0:T(8,128)(2,1)S(1)}, u32[]{:S(2)}, u32[]{:S(2)}) collective-permute-start(bf16[3,128,384]{2,1,0:T(8,128)(2,1)S(1)} %get-tuple-element.114), channel_id=1, source_target_pairs={{1,0},{2,1},{3,2},{4,3},{5,4},{6,5},{7,6},{8,7},{9,8},{10,9},{11,1... | collective-permute-start | bytes 884744 | tf_op jit(solution)/shard_map/ppermute | solution.py:15
  4.5 8.8 %collective-permute-start = (bf16[3,128,384]{2,1,0:T(8,128)(2,1)S(1)}, bf16[3,128,384]{2,1,0:T(8,128)(2,1)S(1)}, u32[]{:S(2)}, u32[]{:S(2)}) collective-permute-start(bf16[3,128,384]{2,1,0:T(8,128)(2,1)S(1)} %get-tuple-element.115), channel_id=1, source_target_pairs={{0,1},{1,2},{2,3},{3,4},{4,5},{5,6},{6,7},{7,8},{8,9},{9,10},{10,1... | collective-permute-start | bytes 884744 | tf_op jit(solution)/shard_map/ppermute | solution.py:14
  25.9 1.9 %copy-start.2 = (f32[8,128,384]{2,1,0:T(8,128)S(1)}, f32[8,128,384]{2,1,0:T(8,128)}, u32[]{:S(2)}) copy-start(f32[8,128,384]{2,1,0:T(8,128)} %get-tuple-element.109) | copy-start | bytes 4718596
  27.8 1.7 %copy-start.13 = (bf16[2,384,1536]{2,1,0:T(8,128)(2,1)S(1)}, bf16[2,384,1536]{2,1,0:T(8,128)(2,1)}, u32[]{:S(2)}) copy-start(bf16[2,384,1536]{2,1,0:T(8,128)(2,1)} %param.16) | copy-start | bytes 7077892
  29.5 2.9 %copy-start.6 = (bf16[8,128,384]{2,1,0:T(8,128)(2,1)S(1)}, bf16[8,128,384]{2,1,0:T(8,128)(2,1)}, u32[]{:S(2)}) copy-start(bf16[8,128,384]{2,1,0:T(8,128)(2,1)} %param.12) | copy-start | bytes 2359300
  29.5 2.9 %copy-start.15 = (bf16[2,384,1536]{2,1,0:T(8,128)(2,1)S(1)}, bf16[2,384,1536]{2,1,0:T(8,128)(2,1)}, u32[]{:S(2)}) copy-start(bf16[2,384,1536]{2,1,0:T(8,128)(2,1)} %param.18) | copy-start | bytes 7077892
  32.4 2.7 %copy-start.8 = (bf16[384,256]{1,0:T(8,128)(2,1)S(1)}, bf16[384,256]{1,0:T(8,128)(2,1)}, u32[]{:S(2)}) copy-start(bf16[384,256]{1,0:T(8,128)(2,1)} %param.19) | copy-start | bytes 589828
  35.1 7.8 %copy-start.18 = (s32[16]{0:T(128)S(1)}, s32[16]{0:T(128)}, u32[]{:S(2)}) copy-start(s32[16]{0:T(128)} %param.21) | copy-start | bytes 196
  35.1 7.9 %copy-start.12 = (s32[128]{0:T(128)S(1)}, s32[128]{0:T(128)}, u32[]{:S(2)}) copy-start(s32[128]{0:T(128)} %param.22) | copy-start | bytes 1540
  36.7 20.4 %all-to-all-start = ((bf16[8,128,256]{2,0,1:T(8,128)(2,1)}), bf16[8,128,256]{2,0,1:T(8,128)(2,1)S(1)}, u32[]{:S(2)}, u32[]{:S(2)}) async-start(bf16[8,128,256]{2,0,1:T(8,128)(2,1)} %copy.22), calls=%async_computation | async-start | bytes 1048576 | tf_op jit(solution)/shard_map/all_to_all | solution.py:48
  57.2 6.0 %copy-start.10 = (s32[8,128]{1,0:T(8,128)S(1)}, s32[8,128]{1,0:T(8,128)}, u32[]{:S(2)}) copy-start(s32[8,128]{1,0:T(8,128)} %param.23) | copy-start | bytes 12292
  57.2 20.1 %copy-start.17 = (bf16[8,128,384]{2,1,0:T(8,128)(2,1)S(1)}, bf16[8,128,384]{2,1,0:T(8,128)(2,1)}, u32[]{:S(2)}) copy-start(bf16[8,128,384]{2,1,0:T(8,128)(2,1)} %param.13) | copy-start | bytes 2359300
  58.8 18.4 %all-to-all-start.1 = ((bf16[128,8,256]{2,1,0:T(8,128)(2,1)}), bf16[128,8,256]{2,1,0:T(8,128)(2,1)S(1)}, u32[]{:S(2)}, u32[]{:S(2)}) async-start(bf16[128,8,256]{2,1,0:T(8,128)(2,1)} %broadcast_select_fusion), calls=%async_computation.1 | async-start | bytes 1048576 | tf_op jit(solution)/shard_map/all_to_all | solution.py:50
  77.7 11.6 %copy-start.3 = (bf16[8,128,384]{2,1,0:T(8,128)(2,1)}, bf16[8,128,384]{2,1,0:T(8,128)(2,1)S(1)}, u32[]{:S(2)}) copy-start(bf16[8,128,384]{2,1,0:T(8,128)(2,1)S(1)} %add_convert_fusion.1) | copy-start | bytes 2359300
  77.8 6.2 %collective-permute-start.2 = (bf16[3,128,384]{2,1,0:T(8,128)(2,1)S(1)}, bf16[3,128,384]{2,1,0:T(8,128)(2,1)S(1)}, u32[]{:S(2)}, u32[]{:S(2)}) collective-permute-start(bf16[3,128,384]{2,1,0:T(8,128)(2,1)S(1)} %get-tuple-element.112), channel_id=1, source_target_pairs={{0,1},{1,2},{2,3},{3,4},{4,5},{5,6},{6,7},{7,8},{8,9},{9,10},{10,1... | collective-permute-start | bytes 884744 | tf_op jit(solution)/shard_map/ppermute | solution.py:14
  80.4 8.6 %collective-permute-start.3 = (bf16[3,128,384]{2,1,0:T(8,128)(2,1)S(1)}, bf16[3,128,384]{2,1,0:T(8,128)(2,1)S(1)}, u32[]{:S(2)}, u32[]{:S(2)}) collective-permute-start(bf16[3,128,384]{2,1,0:T(8,128)(2,1)S(1)} %get-tuple-element.113), channel_id=1, source_target_pairs={{1,0},{2,1},{3,2},{4,3},{5,4},{6,5},{7,6},{8,7},{9,8},{10,9},{11,1... | collective-permute-start | bytes 884744 | tf_op jit(solution)/shard_map/ppermute | solution.py:15
  101.3 1.9 %copy-start.1 = (f32[8,128,384]{2,1,0:T(8,128)S(1)}, f32[8,128,384]{2,1,0:T(8,128)}, u32[]{:S(2)}) copy-start(f32[8,128,384]{2,1,0:T(8,128)} %get-tuple-element.105) | copy-start | bytes 4718596
  103.2 1.7 %copy-start.14 = (bf16[2,384,1536]{2,1,0:T(8,128)(2,1)S(1)}, bf16[2,384,1536]{2,1,0:T(8,128)(2,1)}, u32[]{:S(2)}) copy-start(bf16[2,384,1536]{2,1,0:T(8,128)(2,1)} %param.16) | copy-start | bytes 7077892
  104.9 2.9 %copy-start.4 = (bf16[8,128,384]{2,1,0:T(8,128)(2,1)S(1)}, bf16[8,128,384]{2,1,0:T(8,128)(2,1)}, u32[]{:S(2)}) copy-start(bf16[8,128,384]{2,1,0:T(8,128)(2,1)} %copy-done.3) | copy-start | bytes 2359300
  104.9 2.9 %copy-start.16 = (bf16[2,384,1536]{2,1,0:T(8,128)(2,1)S(1)}, bf16[2,384,1536]{2,1,0:T(8,128)(2,1)}, u32[]{:S(2)}) copy-start(bf16[2,384,1536]{2,1,0:T(8,128)(2,1)} %param.18) | copy-start | bytes 7077892
  (1 other events, 0.9 us)
where the time goes:
time: 112 us; the launch traced here: 110 us
  waiting for transfers between devices  38.5 us (34%)
  other arithmetic  30.1 us (27%)
  starting transfers between devices  20.8 us (19%)
  matrix products  11.2 us (10%)
  local copies, waits for them, and re-layouts  8.78 us (8%)
    reduce_sum x2, other arithmetic, conv_norm(): center = jnp.mean(total, axis=-1, keepdims=True)  23.9 us
    all_to_all x1, waiting for transfers between devices, partner_move(): lax.all_to_all(picked, 'band', split_axis=0, concat_axis=1, tiled=True)  14.1 us
    all_to_all x1, waiting for transfers between devices, partner_move(): lax.all_to_all(tile, 'band', split_axis=1, concat_axis=0, tiled=True)  13.9 us
    all_to_all x1, starting transfers between devices, partner_move(): lax.all_to_all(tile, 'band', split_axis=1, concat_axis=0, tiled=True)  6.25 us
    dot_general x2, matrix products, mixer(): jnp.dot(normed, w_up[which], preferred_element_type=jnp.float32)  5.77 us
    ppermute x2, starting transfers between devices, with_halo(): before = lax.ppermute(last, axis, up)  5.59 us
    ppermute x2, waiting for transfers between devices, with_halo(): before = lax.ppermute(last, axis, up)  5.56 us
    ppermute x2, waiting for transfers between devices, with_halo(): after = lax.ppermute(first, axis, down)  4.98 us
  transfers between devices with their start and end apart: 6, of which 5 were waited for; matrix products, arithmetic and copies ran while one was open for 2% of the time, Pallas kernels for 0%

commit v1 on v0

v1 whole, which is shorter than its diff:
```python
import functools

import jax
import jax.numpy as jnp
from jax import lax
from jax.experimental import pallas as pl
from jax.experimental.pallas import tpu as pltpu
from jax.sharding import PartitionSpec as P

LANES = 128
SUB = 8
TAPS = 7
PAD = TAPS // 2
TILE = 256
F32 = jnp.float32
BF16 = jnp.bfloat16
VMEM = pl.BlockSpec(memory_space=pltpu.VMEM)
ANY = pl.BlockSpec(memory_space=pl.ANY)
LIMIT = 24 << 20


def far(x):
    return pltpu.with_memory_space_constraint(x, pltpu.HBM)


def near(x):
    return pltpu.with_memory_space_constraint(x, pltpu.VMEM)


class Plan:
    def __init__(self, rows, taps):
        self.z_ops, self.k_ops, self.leaves = [], [], []
        self.z_index, self.k_index = {}, {}
        zs = [self.z(("row", m)) for m in range(rows + taps - 1)]
        ks = [self.k(("tap", a)) for a in range(taps)]
        self.outs = self.fast(zs, ks, rows)

    def z(self, op):
        if op not in self.z_index:
            self.z_index[op] = len(self.z_ops)
            self.z_ops.append(op)
        return self.z_index[op]

    def k(self, op):
        if op not in self.k_index:
            self.k_index[op] = len(self.k_ops)
            self.k_ops.append(op)
        return self.k_index[op]

    def leaf(self, z, k):
        self.leaves.append((z, k))
        return ("leaf", len(self.leaves) - 1)

    def fast(self, zs, ks, count):
        if count % 2 or len(ks) == 1:
            outs = []
            for i in range(count):
                node = self.leaf(zs[i], ks[0])
                for j in range(1, len(ks)):
                    node = ("add", node, self.leaf(zs[i + j], ks[j]))
                outs.append(node)
            return outs
        half = count // 2
        even, odd, k0, k1 = zs[0::2], zs[1::2], ks[0::2], ks[1::2]
        both = [self.k(("add", k0[j], k1[j])) if j < len(k1) else k0[j] for j in range(len(k0))]
        need = half + len(k0) - 1
        first = self.fast(odd[:need], both, half)
        second = self.fast([self.z(("sub", even[n], odd[n])) for n in range(need)], k0, half)
        need = half + len(k1) - 1
        third = self.fast([self.z(("sub", even[n + 1], odd[n])) for n in range(need)], k1, half)
        outs = []
        for n in range(half):
            outs += [("add", first[n], second[n]), ("add", first[n], third[n])]
        return outs

    def rows_of(self, z):
        op = self.z_ops[z]
        return {op[1]} if op[0] == "row" else self.rows_of(op[1]) | self.rows_of(op[2])

    def split(self, known):
        early = [q for q, (z, _) in enumerate(self.leaves) if self.rows_of(z) <= set(known)]
        return early, [q for q in range(len(self.leaves)) if q not in early]


def tap_rows(kernel_ref, which, plan, leaves, weights):
    values = []
    for op in plan.k_ops:
        if op[0] == "tap":
            values.append(kernel_ref[op[1], :, which, :])
        else:
            values.append(values[op[1]] + values[op[2]])
    for n, q in enumerate(leaves):
        weights[n, 0:TAPS, :] = values[plan.leaves[q][1]]


def fill(load, plan, leaves, derived, width, lane_blocks):
    last = width // SUB - 1
    for block in range(width // SUB):
        for cb in range(lane_blocks):
            values = {}

            def node(z):
                if z not in values:
                    op = plan.z_ops[z]
                    if op[0] == "row":
                        values[z] = load(op[1], block, cb).astype(F32)
                    else:
                        values[z] = node(op[1]) - node(op[2])
                return values[z]

            for n, q in enumerate(leaves):
                value = node(plan.leaves[q][0])
                derived[cb, n, (block + 1) * SUB : (block + 2) * SUB, :] = value
                if block == 0:
                    derived[cb, n, width + SUB : width + 2 * SUB, :] = value
                if block == last:
                    derived[cb, n, 0:SUB, :] = value


def fir(derived, weights, cb, n, start, wide):
    lanes = slice(cb * LANES, (cb + 1) * LANES)
    total = [None] * wide
    for b in range(TAPS):
        weight = jnp.broadcast_to(weights[n, b : b + 1, lanes], (SUB, LANES))
        for v in range(wide):
            term = weight * derived[cb, n, pl.ds(start + (SUB - PAD + b + v * SUB), SUB), :]
            total[v] = term if total[v] is None else total[v] + term
    return total


def early_kernel(which, *refs):
    x_ref, kernel_hbm, early_ref, kernel, derived, weights, sem = refs
    rows, width, channels = x_ref.shape
    lane_blocks = channels // LANES
    plan = Plan(rows, TAPS)
    leaves, _ = plan.split(range(PAD, PAD + rows))
    copy = pltpu.make_async_copy(kernel_hbm, kernel, sem)
    copy.start()

    def load(m, block, cb):
        return x_ref[m - PAD, block * SUB : (block + 1) * SUB, cb * LANES : (cb + 1) * LANES]

    fill(load, plan, leaves, derived, width, lane_blocks)
    copy.wait()
    tap_rows(kernel, which, plan, leaves, weights)
    wide = 2 if width % (2 * SUB) == 0 else 1
    for cb in range(lane_blocks):

        @pl.loop(0, width // (wide * SUB))
        def _(step):
            start = pl.multiple_of(step * (wide * SUB), wide * SUB)
            for n in range(len(leaves)):
                for v, part in enumerate(fir(derived, weights, cb, n, start, wide)):
                    early_ref[cb, n, pl.ds(start + v * SUB, SUB), :] = part


def early(which, x, kernel):
    rows, width, channels = x.shape
    plan = Plan(rows, TAPS)
    leaves, _ = plan.split(range(PAD, PAD + rows))
    blocks = channels // LANES
    return pl.pallas_call(
        functools.partial(early_kernel, which),
        out_shape=pltpu.VMEM((blocks, len(leaves), width, LANES), F32),
        in_specs=[VMEM, ANY],
        out_specs=VMEM,
        scratch_shapes=[
            pltpu.VMEM(kernel.shape, F32),
            pltpu.VMEM((blocks, len(leaves), width + 2 * SUB, LANES), F32),
            pltpu.VMEM((len(leaves), SUB, channels), F32),
            pltpu.SemaphoreType.DMA,
        ],
        compiler_params=pltpu.CompilerParams(vmem_limit_bytes=12 << 20),
        cost_estimate=pl.CostEstimate(
            flops=40 * rows * width * channels, bytes_accessed=8 * rows * width * channels, transcendentals=0
        ),
        name=f"early{which}",
    )(near(x), far(kernel))


def gelu(u):
    half = 0.5 * u
    return half + half * jnp.tanh(u * (0.7978845608028654 + 0.035677408136300125 * (u * u)))


def mix_kernel(cfg, *refs):
    which, has_flux, split, prefetch = cfg
    refs = list(refs)
    x_ref, early_ref, one_ref, two_ref, odd_ref = [refs.pop(0) for _ in range(5)]
    kernel_hbm, gain_hbm, wu_hbm, bu_hbm, wd_hbm = [refs.pop(0) for _ in range(5)]
    fo_hbm = refs.pop(0) if has_flux else None
    sources = [refs.pop(0) for _ in range(prefetch)]
    out_hbm = refs.pop(0)
    surf_hbm = refs.pop(0) if has_flux else None
    targets = [refs.pop(0) for _ in range(prefetch)]
    kernel, gain, wu, bu, wd, derived, weights, conv, hidden, out, sem = refs[:11]
    rows, width, channels = x_ref.shape
    lane_blocks = channels // LANES
    plan = Plan(rows, TAPS)
    known, leaves = plan.split(range(PAD, PAD + rows))

    load_kernel = pltpu.make_async_copy(kernel_hbm, kernel, sem.at[0])
    late = [
        pltpu.make_async_copy(gain_hbm, gain, sem.at[1]),
        pltpu.make_async_copy(bu_hbm, bu, sem.at[2]),
        pltpu.make_async_copy(wu_hbm.at[which], wu, sem.at[3]),
        pltpu.make_async_copy(wd_hbm.at[which], wd, sem.at[4]),
    ]
    if has_flux:
        fo, surf = refs[11:]
        late.append(pltpu.make_async_copy(fo_hbm, fo, sem.at[5]))
    ahead = [
        pltpu.make_async_copy(source, target, sem.at[6 + n])
        for n, (source, target) in enumerate(zip(sources, targets))
    ]
    load_kernel.start()
    for copy in late + ahead:
        copy.start()

    odd = odd_ref[0] == 1

    def load(m, block, cb):
        lons, lanes = slice(block * SUB, (block + 1) * SUB), slice(cb * LANES, (cb + 1) * LANES)
        if PAD <= m < PAD + rows:
            return x_ref[m - PAD, lons, lanes]
        r = m if m < PAD else m - PAD - rows
        one, two = one_ref[r, lons, lanes].astype(F32), two_ref[r, lons, lanes].astype(F32)
        return jnp.where(odd, one, two) if m < PAD else jnp.where(odd, two, one)

    fill(load, plan, leaves, derived, width, lane_blocks)
    load_kernel.wait()
    tap_rows(kernel, which, plan, leaves, weights)
    wide = 2 if width % (2 * SUB) == 0 else 1
    for cb in range(lane_blocks):
        lanes = slice(cb * LANES, (cb + 1) * LANES)

        @pl.loop(0, width // (wide * SUB))
        def _(step):
            start = pl.multiple_of(step * (wide * SUB), wide * SUB)
            done = {}

            def value(node):
                if node not in done:
                    if node[0] == "add":
                        left, right = value(node[1]), value(node[2])
                        done[node] = [a + b for a, b in zip(left, right)]
                    elif node[1] in known:
                        n = known.index(node[1])
                        done[node] = [
                            early_ref[cb, n, pl.ds(start + v * SUB, SUB), :] for v in range(wide)
                        ]
                    else:
                        done[node] = fir(derived, weights, cb, leaves.index(node[1]), start, wide)
                return done[node]

            for i, node in enumerate(plan.outs):
                for v, part in enumerate(value(node)):
                    conv[i, pl.ds(start + v * SUB, SUB), lanes] = part

    for copy in late:
        copy.wait()
    group = rows // 2 if rows % 2 == 0 else rows
    cells = group * width
    stores = []
    for g in range(rows // group):
        part = slice(g * group, (g + 1) * group)
        total = conv[part].reshape(cells, channels)
        center = jnp.mean(total, axis=-1, keepdims=True)
        total = total - center
        spread = jnp.mean(total * total, axis=-1, keepdims=True)
        normed = (total * lax.rsqrt(spread + 1e-6) * gain[which : which + 1, :]).astype(BF16)
        for n in range(hidden.shape[1] // TILE):
            cols = slice(n * TILE, (n + 1) * TILE)
            u = jnp.dot(normed, wu[:, cols], preferred_element_type=F32)
            hidden[g * cells : (g + 1) * cells, cols] = gelu(u + bu[which : which + 1, cols]).astype(BF16)
        update = lax.dot_general(
            hidden[g * cells : (g + 1) * cells, :], wd[...], (((1,), (1,)), ((), ())), preferred_element_type=F32
        ).reshape(group, width, channels)
        result = (x_ref[part].astype(F32) + update).astype(BF16)
        out[part] = result
        at = pl.ds(g * group, group)
        stores.append(pltpu.make_async_copy(out.at[at], out_hbm.at[at], sem.at[16 + 2 * g]))
        stores[-1].start()
        if has_flux:
            flux = jnp.dot(result.reshape(cells, channels), fo[...], preferred_element_type=F32).astype(BF16)
            if split:
                for i in range(group):
                    piece = flux[i * width : (i + 1) * width].reshape(split, width // split, flux.shape[1])
                    surf[:, g * group + i] = piece
                store = pltpu.make_async_copy(surf.at[:, at], surf_hbm.at[:, at], sem.at[17 + 2 * g])
            else:
                surf[part] = flux.reshape(group, width, flux.shape[1])
                store = pltpu.make_async_copy(surf.at[at], surf_hbm.at[at], sem.at[17 + 2 * g])
            store.start()
            stores.append(store)
    for copy in ahead + stores:
        copy.wait()


def mix(which, x, known, halo, shared, flux_out=None, split=0, prefetch=()):
    kernel, gain, w_up, b_up, w_down = shared
    one, two, odd = halo
    rows, width, channels = x.shape
    has_flux = flux_out is not None
    cells = rows * width
    hidden = w_up.shape[-1]
    args = [near(x), near(known), near(one), near(two), odd]
    specs = [VMEM] * 4 + [pl.BlockSpec(memory_space=pltpu.SMEM)]
    far_args = [kernel, gain, w_up, b_up, w_down]
    out_shape = [jax.ShapeDtypeStruct((rows, width, channels), BF16)]
    out_specs = [ANY]
    plan = Plan(rows, TAPS)
    _, leaves = plan.split(range(PAD, PAD + rows))
    scratch = [
        pltpu.VMEM(kernel.shape, F32),
        pltpu.VMEM(gain.shape, F32),
        pltpu.VMEM(w_up.shape[1:], BF16),
        pltpu.VMEM(b_up.shape, F32),
        pltpu.VMEM(w_down.shape[1:], BF16),
        pltpu.VMEM((channels // LANES, len(leaves), width + 2 * SUB, LANES), F32),
        pltpu.VMEM((len(leaves), SUB, channels), F32),
        pltpu.VMEM((rows, width, channels), F32),
        pltpu.VMEM((cells, hidden), BF16),
        pltpu.VMEM((rows, width, channels), BF16),
        pltpu.SemaphoreType.DMA((32,)),
    ]
    if has_flux:
        far_args.append(flux_out)
        depth = flux_out.shape[1]
        shape = (split, rows, width // split, depth) if split else (rows, width, depth)
        out_shape.append(jax.ShapeDtypeStruct(shape, BF16))
        out_specs.append(ANY)
        scratch += [pltpu.VMEM(flux_out.shape, BF16), pltpu.VMEM(shape, BF16)]
    far_args += prefetch
    out_shape += [pltpu.VMEM(v.shape, v.dtype) for v in prefetch]
    out_specs += [VMEM] * len(prefetch)
    args += [far(v) for v in far_args]
    specs += [ANY] * len(far_args)
    return pl.pallas_call(
        functools.partial(mix_kernel, (which, has_flux, split, len(prefetch))),
        out_shape=out_shape,
        in_specs=specs,
        out_specs=out_specs,
        scratch_shapes=scratch,
        compiler_params=pltpu.CompilerParams(vmem_limit_bytes=LIMIT),
        cost_estimate=pl.CostEstimate(
            flops=4 * cells * channels * hidden, bytes_accessed=14 * cells * channels, transcendentals=cells * hidden
        ),
        name=f"mix{which}",
    )(*args)


def ocean_in_kernel(split, ocean_ref, moved_ref, mask_ref, fi_ref, out_ref, first_ref, last_ref):
    rows, width, channels = out_ref.shape
    mask = jnp.transpose(mask_ref[...].astype(F32))
    order = list(range(PAD)) + list(range(rows - PAD, rows)) + list(range(PAD, rows - PAD))
    for i in order:
        moved = moved_ref[:, i].reshape(width, fi_ref.shape[0]) if split else moved_ref[i]
        forcing = jnp.dot(moved, fi_ref[...], preferred_element_type=F32)
        value = (ocean_ref[i].astype(F32) + mask[:, i : i + 1] * forcing).astype(BF16)
        out_ref[i] = value
        if i < PAD:
            first_ref[i] = value
        if i >= rows - PAD:
            last_ref[i - rows + PAD] = value


def ocean_input(ocean, moved, mask, flux_in, split):
    rows, width, channels = ocean.shape
    shapes = [(rows, width, channels), (PAD, width, channels), (PAD, width, channels)]
    return pl.pallas_call(
        functools.partial(ocean_in_kernel, split),
        out_shape=[pltpu.VMEM(shape, BF16) for shape in shapes],
        in_specs=[VMEM] * 4,
        out_specs=[VMEM] * 3,
        compiler_params=pltpu.CompilerParams(vmem_limit_bytes=8 << 20),
        cost_estimate=pl.CostEstimate(
            flops=2 * rows * width * channels * flux_in.shape[0], bytes_accessed=8 * rows * width * channels, transcendentals=0
        ),
        name="ocean_in",
    )(near(ocean), near(moved), near(mask), near(flux_in))


def halos(first, last):
    size = lax.axis_size("band")
    odd = lax.axis_index("band") % 2
    inner = [(i, i ^ 1) for i in range(size)]
    outer = [(i, i + 1) for i in range(1, size - 1, 2)] + [(i + 1, i) for i in range(1, size - 1, 2)]
    one = lax.ppermute(jnp.where(odd == 1, first, last), "band", inner)
    two = lax.ppermute(jnp.where(odd == 1, last, first), "band", outer)
    return one, two, odd.astype(jnp.int32).reshape(1)


def per_device(
    atm_state,
    ocean_state,
    dw_kernel,
    norm_gain,
    w_up,
    b_up,
    w_down,
    flux_out,
    flux_in,
    partner,
    remap,
    land_mask,
):
    height, width, channels = atm_state.shape
    size = lax.axis_size("band")
    share = width // size
    split = size if share % SUB == 0 else 0
    band_rows = remap.shape[0] // partner.shape[0]
    indices = jnp.repeat(partner, band_rows) * band_rows + remap
    shared = (dw_kernel.transpose(1, 2, 0, 3), norm_gain, w_up, b_up, w_down)

    halo = halos(atm_state[:PAD], atm_state[-PAD:])
    known = early(0, atm_state, shared[0])
    atm_next, surface, ocean, mask, fi = mix(
        0, atm_state, known, halo, shared, flux_out, split, (ocean_state, land_mask, flux_in)
    )
    if not split:
        surface = surface.reshape(height, size, share, -1).transpose(1, 0, 2, 3)
    spread = lax.all_to_all(surface, "band", split_axis=0, concat_axis=0, tiled=True)
    picked = jnp.take(spread.reshape((size * height,) + spread.shape[2:]), indices, axis=0, mode="clip")
    moved = lax.all_to_all(picked.reshape(spread.shape), "band", split_axis=0, concat_axis=0, tiled=True)
    if not split:
        moved = moved.transpose(1, 0, 2, 3).reshape(height, width, -1)
    ocean_in, first, last = ocean_input(ocean, moved, mask, fi, split)
    halo = halos(first, last)
    known = early(1, ocean_in, shared[0])
    (ocean_next,) = mix(1, ocean_in, known, halo, shared)
    return (atm_next, ocean_next)


def solution(mesh):
    in_specs = (
        P(("ens", "band"), None, None),
        P(("ens", "band"), None, None),
        P(),
        P(),
        P(),
        P(),
        P(),
        P(),
        P(),
        P("ens"),
        P("ens"),
        P(("ens", "band"), None),
    )
    out_specs = (P(("ens", "band"), None, None), P(("ens", "band"), None, None))
    return jax.shard_map(
        per_device, mesh=mesh, in_specs=in_specs, out_specs=out_specs, check_vma=False
    )
```

time: 112 us -> 80.8 us (0.72); the launches traced: 110 us -> 80.4 us
  other arithmetic: 30.1 us -> 1.26 us
  Pallas kernels: 0 us -> 22.8 us
  blocking collectives: 0 us -> 18.2 us
  waiting for transfers between devices: 38.5 us -> 22.7 us
  matrix products: 11.2 us -> 0 us
  starting transfers between devices: 20.8 us -> 12.5 us
  local copies, waits for them, and re-layouts: 8.78 us -> 1.95 us
    reduce_sum x4 -> x0, other arithmetic: 27.7 us -> none  [the longest x2 23.9 us: conv_norm(): center = jnp.mean(total, axis=-1, keepdims=True)]
    pallas_call x0 -> x5, Pallas kernels: none -> 22.8 us  [the longest x2 16.9 us: mix(): pl.pallas_call(functools.partial(mix_kernel, (which, has_flux, split, len...]
    all_to_all x0 -> x1, blocking collectives: none -> 18.2 us  [per_device(): lax.all_to_all(picked.reshape(spread.shape), 'band', split_axis=0, concat...]
    all_to_all x2 -> x1, waiting for transfers between devices: 28 us -> 13.9 us  [per_device(): lax.all_to_all(surface, 'band', split_axis=0, concat_axis=0, tiled=True)]
    dot_general x6 -> x0, matrix products: 11.2 us -> none  [the longest x2 5.77 us: mixer(): jnp.dot(normed, w_up[which], preferred_element_type=jnp.float32)]
    all_to_all x2 -> x1, starting transfers between devices: 10.6 us -> 5.49 us  [per_device(): lax.all_to_all(surface, 'band', split_axis=0, concat_axis=0, tiled=True)]
    ppermute x4, starting transfers between devices: 10.3 us -> 7.03 us  [the longest x2 6.43 us: halos(): two = lax.ppermute(jnp.where(odd == 1, last, first), 'band', outer)]
    slice x12 -> x0, local copies, waits for them, and re-layouts: 3 us -> none  [the longest x1 1.19 us: with_halo(): first = lax.slice_in_dim(array, 0, width, axis=dim)]
  transfers between devices with their start and end apart: 6 -> 5, of which waited for: 5 -> 3; matrix products, arithmetic and copies ran while one was open for 2% -> 0% of each run, Pallas kernels for 0% -> 7%
where the time goes in v1:
time: 80.8 us; the launch traced here: 80.4 us
  Pallas kernels  22.8 us (28%)
  waiting for transfers between devices  22.7 us (28%)
  blocking collectives  18.2 us (23%)
  starting transfers between devices  12.5 us (15%)
  local copies, waits for them, and re-layouts  1.95 us (2%)
  other arithmetic  1.26 us (2%)
  between operations  0.95 us (1%)
    all_to_all x1, blocking collectives, per_device(): lax.all_to_all(picked.reshape(spread.shape), 'band', split_axis=0, concat...  18.2 us
    pallas_call x2, Pallas kernels, mix(): pl.pallas_call(functools.partial(mix_kernel, (which, has_flux, split, len...  16.9 us
    all_to_all x1, waiting for transfers between devices, per_device(): lax.all_to_all(surface, 'band', split_axis=0, concat_axis=0, tiled=True)  13.9 us
    ppermute x2, waiting for transfers between devices, halos(): two = lax.ppermute(jnp.where(odd == 1, last, first), 'band', outer)  8.76 us
    ppermute x2, starting transfers between devices, halos(): two = lax.ppermute(jnp.where(odd == 1, last, first), 'band', outer)  6.43 us
    all_to_all x1, starting transfers between devices, per_device(): lax.all_to_all(surface, 'band', split_axis=0, concat_axis=0, tiled=True)  5.49 us
    pallas_call x2, Pallas kernels, early(): pl.pallas_call(functools.partial(early_kernel, which), out_shape=pltpu.VM...  5.48 us
  transfers between devices with their start and end apart: 5, of which 3 were waited for; matrix products, arithmetic and copies ran while one was open for 0% of the time, Pallas kernels for 7%

profile of v1, /device:TPU:9, one launch (start us, length us, event | category | flops | bytes accessed | tf_op | source)
XLA Modules:
  0.0 80.4 jit_solution(8009574525244434185)
XLA Ops:
  0.6 0.0 copy-start.1
  0.7 1.2 %broadcast_select_fusion.2 = (bf16[3,128,384]{2,1,0:T(8,128)(2,1)S(1)}, bf16[3,128,384]{2,1,0:T(8,128)(2,1)S(1)}) fusion(pred[]{:T(512)S(6)} %eq.5, bf16[8,128,384]{2,1,0:T(8,128)(2,1)} %refs_0_.3), kind=kLoop, calls=%fused_computation.3 | loop fusion | flops 294912 | bytes 1179649 | tf_op jit(solution)/shard_map/jit(_where)/select_n | solution.py:390
  1.8 3.7 %collective-permute-start.1 = (bf16[3,128,384]{2,1,0:T(8,128)(2,1)S(1)}, bf16[3,128,384]{2,1,0:T(8,128)(2,1)S(1)}, u32[]{:S(2)}, u32[]{:S(2)}) collective-permute-start(bf16[3,128,384]{2,1,0:T(8,128)(2,1)S(1)} %get-tuple-element.18), channel_id=1, source_target_pairs={{1,2},{3,4},{5,6},{7,8},{9,10},{11,12},{13,14},{2,1},{4,3},{6,5},{... | collective-permute-start | bytes 884744 | tf_op jit(solution)/shard_map/ppermute | solution.py:390
  5.6 0.1 collective-permute-start
  5.6 0.0 copy-start
  5.6 1.1 %copy-done = bf16[8,128,384]{2,1,0:T(8,128)(2,1)S(1)} copy-done((bf16[8,128,384]{2,1,0:T(8,128)(2,1)S(1)}, bf16[8,128,384]{2,1,0:T(8,128)(2,1)}, u32[]{:S(2)}) %copy-start) | copy-done | bytes 786456
  6.8 2.7 %early0.1.refs_1_ = f32[3,13,128,128]{3,2,1,0:T(8,128)S(1)} custom-call(bf16[8,128,384]{2,1,0:T(8,128)(2,1)S(1)} %copy-done, f32[7,7,2,384]{3,2,1,0:T(2,128)} %bitcast.4), custom_call_target="tpu_custom_call" | custom-call | flops 15728640 | bytes 3145728 | tf_op jit(solution)/shard_map/early0/pallas_call | solution.py:162
  9.5 3.6 %collective-permute-done.1.refs_3_ = bf16[3,128,384]{2,1,0:T(8,128)(2,1)S(1)} collective-permute-done((bf16[3,128,384]{2,1,0:T(8,128)(2,1)S(1)}, bf16[3,128,384]{2,1,0:T(8,128)(2,1)S(1)}, u32[]{:S(2)}, u32[]{:S(2)}) %collective-permute-start.1) | collective-permute-done | bytes 294944 | tf_op jit(solution)/shard_map/ppermute | solution.py:390
  13.1 0.0 collective-permute-done.refs_2_
  13.1 0.0 copy-start.3
  13.1 8.5 %mix0.1 = (bf16[8,128,384]{2,1,0:T(8,128)(2,1)}, bf16[16,8,8,256]{3,2,1,0:T(8,128)(2,1)}, bf16[8,128,384]{2,1,0:T(8,128)(2,1)S(1)}, s32[8,128]{1,0:T(8,128)S(1)}, bf16[256,384]{1,0:T(8,128)(2,1)S(1)}) custom-call(bf16[8,128,384]{2,1,0:T(8,128)(2,1)S(1)} %copy-done.1, f32[3,13,128,128]{3,2,1,0:T(8,128)S(1)} %early0.1.refs_1_, ...), custom_call_target="tpu_custom_call" | custom-call | flops 2415919104 | bytes 5505024 | tf_op jit(solution)/shard_map/mix0/pallas_call | solution.py:339
  21.6 5.5 %all-to-all-start = ((bf16[16,8,8,256]{3,2,1,0:T(8,128)(2,1)}), bf16[16,8,8,256]{3,2,1,0:T(8,128)(2,1)S(1)}, u32[]{:S(2)}, u32[]{:S(2)}) async-start(bf16[16,8,8,256]{3,2,1,0:T(8,128)(2,1)} %get-tuple-element.12), calls=%async_computation | async-start | bytes 1048576 | tf_op jit(solution)/shard_map/all_to_all | solution.py:423
  27.1 0.1 broadcast_in_dim.7
  27.2 0.1 mul.12
  27.3 13.9 %all-to-all-done = bf16[16,8,8,256]{3,2,1,0:T(8,128)(2,1)S(1)} async-done(((bf16[16,8,8,256]{3,2,1,0:T(8,128)(2,1)}), bf16[16,8,8,256]{3,2,1,0:T(8,128)(2,1)S(1)}, u32[]{:S(2)}, u32[]{:S(2)}) %all-to-all-start) | async-done | bytes 524320 | tf_op jit(solution)/shard_map/all_to_all | solution.py:423
  41.2 0.6 gather_fusion
  41.9 18.2 %all_to_all.10.moved_ref = bf16[16,8,8,256]{3,2,1,0:T(8,128)(2,1)S(1)} all-to-all(bf16[16,8,8,256]{3,2,1,0:T(8,128)(2,1)S(1)} %bitcast.9), channel_id=1, replica_groups=mesh['ens'=2,'band'=16] {'band'}, dimensions={0} | all-to-all | bytes 1048576 | tf_op jit(solution)/shard_map/all_to_all | solution.py:425
  60.1 0.5 ocean_in.1
  60.6 0.1 broadcast_select_fusion
  60.7 2.7 %collective-permute-start.3 = (bf16[3,128,384]{2,1,0:T(8,128)(2,1)S(1)}, bf16[3,128,384]{2,1,0:T(8,128)(2,1)S(1)}, u32[]{:S(2)}, u32[]{:S(2)}) collective-permute-start(bf16[3,128,384]{2,1,0:T(8,128)(2,1)S(1)} %get-tuple-element.20), channel_id=1, source_target_pairs={{1,2},{3,4},{5,6},{7,8},{9,10},{11,12},{13,14},{2,1},{4,3},{6,5},{... | collective-permute-start | bytes 884744 | tf_op jit(solution)/shard_map/ppermute | solution.py:390
  63.4 0.5 collective-permute-start.2
  63.9 2.7 %early1.1.refs_1_ = f32[3,13,128,128]{3,2,1,0:T(8,128)S(1)} custom-call(bf16[8,128,384]{2,1,0:T(8,128)(2,1)S(1)} %get-tuple-element.15.refs_0_, f32[7,7,2,384]{3,2,1,0:T(2,128)} %bitcast.6), custom_call_target="tpu_custom_call" | custom-call | flops 15728640 | bytes 3145728 | tf_op jit(solution)/shard_map/early1/pallas_call | solution.py:162
  66.7 5.2 %collective-permute-done.3.refs_3_ = bf16[3,128,384]{2,1,0:T(8,128)(2,1)S(1)} collective-permute-done((bf16[3,128,384]{2,1,0:T(8,128)(2,1)S(1)}, bf16[3,128,384]{2,1,0:T(8,128)(2,1)S(1)}, u32[]{:S(2)}, u32[]{:S(2)}) %collective-permute-start.3) | collective-permute-done | bytes 294944 | tf_op jit(solution)/shard_map/ppermute | solution.py:390
  71.9 8.4 %mix1.1 = bf16[8,128,384]{2,1,0:T(8,128)(2,1)} custom-call(bf16[8,128,384]{2,1,0:T(8,128)(2,1)S(1)} %get-tuple-element.15.refs_0_, f32[3,13,128,128]{3,2,1,0:T(8,128)S(1)} %early1.1.refs_1_, bf16[3,128,384]{2,1,0:T(8,128)(2,1)S(1)} %collective-permute-done.2.refs_2_, bf16[3,128,384]{2,1,0:T(8,128)(2,1)S(1)} %collective-permute-done.3.refs_3_, ...), custom_call_target="tpu_custom_call" | custom-call | flops 2415919104 | bytes 5505024 | tf_op jit(solution)/shard_map/mix1/pallas_call | solution.py:339
  (8 shorter events, 0.0 us)
Async XLA Ops:
  0.6 12.5 %copy-start.1 = (bf16[8,128,384]{2,1,0:T(8,128)(2,1)S(1)}, bf16[8,128,384]{2,1,0:T(8,128)(2,1)}, u32[]{:S(2)}) copy-start(bf16[8,128,384]{2,1,0:T(8,128)(2,1)} %refs_0_.3) | copy-start | bytes 2359300
  1.8 11.3 %collective-permute-start.1 = (bf16[3,128,384]{2,1,0:T(8,128)(2,1)S(1)}, bf16[3,128,384]{2,1,0:T(8,128)(2,1)S(1)}, u32[]{:S(2)}, u32[]{:S(2)}) collective-permute-start(bf16[3,128,384]{2,1,0:T(8,128)(2,1)S(1)} %get-tuple-element.18), channel_id=1, source_target_pairs={{1,2},{3,4},{5,6},{7,8},{9,10},{11,12},{13,14},{2,1},{4,3},{6,5},{... | collective-permute-start | bytes 884744 | tf_op jit(solution)/shard_map/ppermute | solution.py:390
  5.6 7.6 %collective-permute-start = (bf16[3,128,384]{2,1,0:T(8,128)(2,1)S(1)}, bf16[3,128,384]{2,1,0:T(8,128)(2,1)S(1)}, u32[]{:S(2)}, u32[]{:S(2)}) collective-permute-start(bf16[3,128,384]{2,1,0:T(8,128)(2,1)S(1)} %get-tuple-element.19), channel_id=1, source_target_pairs={{0,1},{1,0},{2,3},{3,2},{4,5},{5,4},{6,7},{7,6},{8,9},{9,8},{10,11... | collective-permute-start | bytes 884744 | tf_op jit(solution)/shard_map/ppermute | solution.py:389
  5.6 1.1 %copy-start = (bf16[8,128,384]{2,1,0:T(8,128)(2,1)S(1)}, bf16[8,128,384]{2,1,0:T(8,128)(2,1)}, u32[]{:S(2)}) copy-start(bf16[8,128,384]{2,1,0:T(8,128)(2,1)} %refs_0_.3) | copy-start | bytes 2359300
  13.1 14.0 %copy-start.2 = (s32[16]{0:T(128)S(1)}, s32[16]{0:T(128)}, u32[]{:S(2)}) copy-start(s32[16]{0:T(128)} %param.21) | copy-start | bytes 196
  13.1 14.2 %copy-start.3 = (s32[128]{0:T(128)S(1)}, s32[128]{0:T(128)}, u32[]{:S(2)}) copy-start(s32[128]{0:T(128)} %param.22) | copy-start | bytes 1540
  21.6 19.6 %all-to-all-start = ((bf16[16,8,8,256]{3,2,1,0:T(8,128)(2,1)}), bf16[16,8,8,256]{3,2,1,0:T(8,128)(2,1)S(1)}, u32[]{:S(2)}, u32[]{:S(2)}) async-start(bf16[16,8,8,256]{3,2,1,0:T(8,128)(2,1)} %get-tuple-element.12), calls=%async_computation | async-start | bytes 1048576 | tf_op jit(solution)/shard_map/all_to_all | solution.py:423
  60.7 11.2 %collective-permute-start.3 = (bf16[3,128,384]{2,1,0:T(8,128)(2,1)S(1)}, bf16[3,128,384]{2,1,0:T(8,128)(2,1)S(1)}, u32[]{:S(2)}, u32[]{:S(2)}) collective-permute-start(bf16[3,128,384]{2,1,0:T(8,128)(2,1)S(1)} %get-tuple-element.20), channel_id=1, source_target_pairs={{1,2},{3,4},{5,6},{7,8},{9,10},{11,12},{13,14},{2,1},{4,3},{6,5},{... | collective-permute-start | bytes 884744 | tf_op jit(solution)/shard_map/ppermute | solution.py:390
  63.4 8.4 %collective-permute-start.2 = (bf16[3,128,384]{2,1,0:T(8,128)(2,1)S(1)}, bf16[3,128,384]{2,1,0:T(8,128)(2,1)S(1)}, u32[]{:S(2)}, u32[]{:S(2)}) collective-permute-start(bf16[3,128,384]{2,1,0:T(8,128)(2,1)S(1)} %get-tuple-element.21), channel_id=1, source_target_pairs={{0,1},{1,0},{2,3},{3,2},{4,5},{5,4},{6,7},{7,6},{8,9},{9,8},{10,11... | collective-permute-start | bytes 884744 | tf_op jit(solution)/shard_map/ppermute | solution.py:389

commit v2 on v0

v2 whole, which is shorter than its diff:
```python
import functools

import jax
import jax.numpy as jnp
from jax import lax
from jax.experimental import pallas as pl
from jax.experimental.pallas import tpu as pltpu
from jax.sharding import PartitionSpec as P

LANES = 128
SUB = 8
TAPS = 7
PAD = TAPS // 2
TILE = 256
F32 = jnp.float32
BF16 = jnp.bfloat16
VMEM = pl.BlockSpec(memory_space=pltpu.VMEM)
ANY = pl.BlockSpec(memory_space=pl.ANY)
LIMIT = 24 << 20


def far(x):
    return pltpu.with_memory_space_constraint(x, pltpu.HBM)


def near(x):
    return pltpu.with_memory_space_constraint(x, pltpu.VMEM)


class Plan:
    def __init__(self, rows, taps):
        self.rows = rows
        self.z_ops, self.k_ops, self.leaves = [], [], []
        self.z_index, self.k_index = {}, {}
        zs = [self.z(("row", m)) for m in range(rows + taps - 1)]
        ks = [self.k(("tap", a)) for a in range(taps)]
        self.outs = self.fast(zs, ks, rows)

    def z(self, op):
        if op not in self.z_index:
            self.z_index[op] = len(self.z_ops)
            self.z_ops.append(op)
        return self.z_index[op]

    def k(self, op):
        if op not in self.k_index:
            self.k_index[op] = len(self.k_ops)
            self.k_ops.append(op)
        return self.k_index[op]

    def leaf(self, z, k):
        self.leaves.append((z, k))
        return ("leaf", len(self.leaves) - 1)

    def fast(self, zs, ks, count):
        if count % 2 or len(ks) == 1:
            outs = []
            for i in range(count):
                node = self.leaf(zs[i], ks[0])
                for j in range(1, len(ks)):
                    node = ("add", node, self.leaf(zs[i + j], ks[j]))
                outs.append(node)
            return outs
        half = count // 2
        even, odd, k0, k1 = zs[0::2], zs[1::2], ks[0::2], ks[1::2]
        both = [self.k(("add", k0[j], k1[j])) if j < len(k1) else k0[j] for j in range(len(k0))]
        need = half + len(k0) - 1
        first = self.fast(odd[:need], both, half)
        second = self.fast([self.z(("sub", even[n], odd[n])) for n in range(need)], k0, half)
        need = half + len(k1) - 1
        third = self.fast([self.z(("sub", even[n + 1], odd[n])) for n in range(need)], k1, half)
        outs = []
        for n in range(half):
            outs += [("add", first[n], second[n]), ("add", first[n], third[n])]
        return outs


def fill(load, rows, products, derived, width, lane_blocks):
    last = width // SUB - 1
    for block in range(width // SUB):
        for cb in range(lane_blocks):
            lons, lanes = slice(block * SUB, (block + 1) * SUB), slice(cb * LANES, (cb + 1) * LANES)
            for n, value in enumerate(rows(lambda m: load(m, lons, lanes).astype(F32))):
                derived[cb, n, (block + 1) * SUB : (block + 2) * SUB, :] = value
                if block == 0:
                    derived[cb, n, width + SUB : width + 2 * SUB, :] = value
                if block == last:
                    derived[cb, n, 0:SUB, :] = value


def fir(derived, weights, cb, z, n, start, wide):
    lanes = slice(cb * LANES, (cb + 1) * LANES)
    total = [None] * wide
    for b in range(TAPS):
        weight = jnp.broadcast_to(weights[n, b : b + 1, lanes], (SUB, LANES))
        for v in range(wide):
            term = weight * derived[cb, z, pl.ds(start + (SUB - PAD + b + v * SUB), SUB), :]
            total[v] = term if total[v] is None else total[v] + term
    return total


def own_rows(plan):
    def rows(load):
        values = {}

        def node(z):
            if z not in values:
                op = plan.z_ops[z]
                if op[0] == "row":
                    inside = PAD <= op[1] < PAD + plan.rows
                    values[z] = load(op[1] - PAD) if inside else None
                else:
                    left, right = node(op[1]), node(op[2])
                    values[z] = left if right is None else (-right if left is None else left - right)
            return values[z]

        return [node(z) for z, _ in plan.leaves]

    return rows


def tap_rows(kernel_ref, which, plan, weights):
    values = []
    for op in plan.k_ops:
        if op[0] == "tap":
            values.append(kernel_ref[op[1], :, which, :])
        else:
            values.append(values[op[1]] + values[op[2]])
    for n, (_, k) in enumerate(plan.leaves):
        weights[n, 0:TAPS, :] = values[k]


EDGE_PRODUCTS = ((3, 1, None), (0, 0, 1), (2, 2, None), (1, 2, 1), (0, 2, None))
EDGE_OUTS = ((0, 1, 2), (0, 3), (4,))


def gelu(u):
    half = 0.5 * u
    return half + half * jnp.tanh(u * (0.7978845608028654 + 0.035677408136300125 * (u * u)))


def expand(which, total, gain, wu, bu, hidden):
    center = jnp.mean(total, axis=-1, keepdims=True)
    total = total - center
    spread = jnp.mean(total * total, axis=-1, keepdims=True)
    normed = (total * lax.rsqrt(spread + 1e-6) * gain[which : which + 1, :]).astype(BF16)
    for n in range(hidden.shape[1] // TILE):
        cols = slice(n * TILE, (n + 1) * TILE)
        u = jnp.dot(normed, wu[:, cols], preferred_element_type=F32)
        hidden[:, cols] = gelu(u + bu[which : which + 1, cols]).astype(BF16)


def contract(split, base, hidden, x_ref, wd, out, flux_refs):
    count, width, channels = out.shape
    update = lax.dot_general(
        hidden[...], wd[...], (((1,), (1,)), ((), ())), preferred_element_type=F32
    )
    for n in range(count):
        out[n] = (x_ref[base + n].astype(F32) + update[n * width : (n + 1) * width]).astype(BF16)
    if flux_refs:
        fo, surf = flux_refs
        flux = jnp.dot(out[...].reshape(count * width, channels), fo[...], preferred_element_type=F32).astype(BF16)
        for n in range(count):
            row = flux[n * width : (n + 1) * width]
            if split:
                surf[:, n] = row.reshape(split, width // split, flux.shape[1])
            else:
                surf[n] = row


def surface_rows(split, ref, first, count):
    return ref.at[:, pl.ds(first, count)] if split else ref.at[pl.ds(first, count)]


def own_kernel(which, *refs):
    x_ref, kernel, *refs = refs
    number = (len(refs) - 4) // 2
    sources, acc_ref, targets = refs[:number], refs[number], refs[number + 1 : 2 * number + 1]
    derived, weights, sem = refs[2 * number + 1 :]
    rows, width, channels = x_ref.shape
    lane_blocks = channels // LANES
    plan = Plan(rows, TAPS)
    copies = [
        pltpu.make_async_copy(source.at[which] if len(source.shape) == 3 else source, target, sem.at[n])
        for n, (source, target) in enumerate(zip(sources, targets))
    ]
    for copy in copies:
        copy.start()
    fill(
        lambda m, lons, lanes: x_ref[m, lons, lanes], own_rows(plan), plan.leaves, derived, width, lane_blocks
    )
    tap_rows(kernel, which, plan, weights)
    wide = 2 if width % (2 * SUB) == 0 else 1
    for cb in range(lane_blocks):
        lanes = slice(cb * LANES, (cb + 1) * LANES)

        @pl.loop(0, width // (wide * SUB))
        def _(step):
            start = pl.multiple_of(step * (wide * SUB), wide * SUB)
            done = {}

            def value(node):
                if node not in done:
                    if node[0] == "add":
                        left, right = value(node[1]), value(node[2])
                        done[node] = [a + b for a, b in zip(left, right)]
                    else:
                        done[node] = fir(derived, weights, cb, node[1], node[1], start, wide)
                return done[node]

            for i, node in enumerate(plan.outs):
                for v, part in enumerate(value(node)):
                    acc_ref[i, pl.ds(start + v * SUB, SUB), lanes] = part

    for copy in copies:
        copy.wait()


def side_kernel(cfg, *refs):
    which, has_flux, split, first, prefetch = cfg
    refs = list(refs)
    x_ref, acc_ref, wu, wd, kernel, gain, bu, halo_ref = [refs.pop(0) for _ in range(8)]
    fo = refs.pop(0) if has_flux else None
    rows, width, channels = x_ref.shape
    middle = rows - 2 * PAD
    held = [refs.pop(0) for _ in range((1 + has_flux) * (not first))]
    odd_ref = refs.pop(0)
    sources = [refs.pop(0) for _ in range(prefetch)]
    surf = None
    if first:
        out = refs.pop(0)
        surf = refs.pop(0) if has_flux else None
        targets = [refs.pop(0) for _ in range(prefetch)]
        derived, weights, conv, hidden, sem = refs
    else:
        out_hbm = refs.pop(0)
        surf_hbm = refs.pop(0) if has_flux else None
        targets = [refs.pop(0) for _ in range(prefetch)]
        derived, weights, conv, hidden, sem, out = refs[:6]
        surf = refs[6] if has_flux else None
    lane_blocks = channels // LANES
    before = odd_ref[0] if first else 1 - odd_ref[0]
    count = PAD + middle if first else PAD
    base = (1 - before) * (rows - count)

    copies = [(source, target) for source, target in zip(sources, targets)]
    if not first:
        place = before * PAD
        copies.append((held[0], out_hbm.at[pl.ds(place, PAD + middle)]))
        if has_flux:
            copies.append((held[1], surface_rows(split, surf_hbm, place, PAD + middle)))
    copies = [pltpu.make_async_copy(a, b, sem.at[n]) for n, (a, b) in enumerate(copies)]
    for copy in copies:
        copy.start()

    def rows_of(load):
        d = [load(before * (PAD - 1 - j) + (1 - before) * j) for j in range(PAD)]
        return d + [d[0] + d[1]]

    def taps(j):
        return kernel[before * (PAD - 1 - j) + (1 - before) * (PAD + 1 + j), :, which, :]

    fill(lambda m, lons, lanes: halo_ref[m, lons, lanes], rows_of, EDGE_PRODUCTS, derived, width, lane_blocks)
    for n, (_, add, subtract) in enumerate(EDGE_PRODUCTS):
        weights[n, 0:TAPS, :] = taps(add) if subtract is None else taps(add) - taps(subtract)
    wide = 2 if width % (2 * SUB) == 0 else 1
    for cb in range(lane_blocks):
        lanes = slice(cb * LANES, (cb + 1) * LANES)

        @pl.loop(0, width // (wide * SUB))
        def _(step):
            start = pl.multiple_of(step * (wide * SUB), wide * SUB)
            done = {}
            for j, products in enumerate(EDGE_OUTS):
                row = before * j + (1 - before) * (rows - 1 - j)
                total = [acc_ref[row, pl.ds(start + v * SUB, SUB), lanes] for v in range(wide)]
                for n in products:
                    if n not in done:
                        done[n] = fir(derived, weights, cb, EDGE_PRODUCTS[n][0], n, start, wide)
                    total = [a + b for a, b in zip(total, done[n])]
                for v in range(wide):
                    conv[row - base, pl.ds(start + v * SUB, SUB), lanes] = total[v]

    if first:
        for n in range(middle):
            conv[before * PAD + n] = acc_ref[PAD + n]
    expand(which, conv[...].reshape(count * width, channels), gain, wu, bu, hidden)
    contract(split, base, hidden, x_ref, wd, out, (fo, surf) if has_flux else None)
    if not first:
        pairs = [(out, out_hbm.at[pl.ds(base, PAD)])]
        if has_flux:
            pairs.append((surf, surface_rows(split, surf_hbm, base, PAD)))
        for a, b in pairs:
            copies.append(pltpu.make_async_copy(a, b, sem.at[len(copies)]))
            copies[-1].start()
    for copy in copies:
        copy.wait()


def mix(which, x, halo, shared, small, flux_out=None, split=0, prefetch=()):
    w_up, w_down = shared
    kernel, gain, b_up = small
    one, two, odd = halo
    rows, width, channels = x.shape
    has_flux = flux_out is not None
    hidden = w_up.shape[-1]
    blocks = channels // LANES
    middle = rows - 2 * PAD
    smem = pl.BlockSpec(memory_space=pltpu.SMEM)

    def piece(count):
        return (split, count, width // split, depth) if split else (count, width, depth)

    def cost(count):
        cells = count * width
        return pl.CostEstimate(
            flops=4 * cells * channels * hidden, bytes_accessed=14 * cells * channels, transcendentals=cells * hidden
        )

    model = [w_up, w_down]
    loaded = [pltpu.VMEM(w_up.shape[1:], BF16), pltpu.VMEM(w_down.shape[1:], BF16)]
    if has_flux:
        depth = flux_out.shape[1]
        model.append(flux_out)
        loaded.append(pltpu.VMEM(flux_out.shape, BF16))
    leaves = len(Plan(rows, TAPS).leaves)
    acc, *loaded = pl.pallas_call(
        functools.partial(own_kernel, which),
        out_shape=[pltpu.VMEM((rows, width, channels), F32)] + loaded,
        in_specs=[VMEM] * 2 + [ANY] * len(model),
        out_specs=[VMEM] * (1 + len(loaded)),
        scratch_shapes=[
            pltpu.VMEM((blocks, leaves, width + 2 * SUB, LANES), F32),
            pltpu.VMEM((leaves, SUB, channels), F32),
            pltpu.SemaphoreType.DMA((4,)),
        ],
        compiler_params=pltpu.CompilerParams(vmem_limit_bytes=16 << 20),
        cost_estimate=pl.CostEstimate(
            flops=60 * rows * width * channels, bytes_accessed=8 * rows * width * channels, transcendentals=0
        ),
        name=f"own{which}",
    )(near(x), near(kernel), *[far(v) for v in model])

    def side(first, halo_rows, held, out_shape, prefetch):
        count = PAD + middle if first else PAD
        close = [x, acc, *loaded[:2], kernel, gain, b_up, halo_rows] + loaded[2:] + held
        scratch = [
            pltpu.VMEM((blocks, PAD + 1, width + 2 * SUB, LANES), F32),
            pltpu.VMEM((len(EDGE_PRODUCTS), SUB, channels), F32),
            pltpu.VMEM((count, width, channels), F32),
            pltpu.VMEM((count * width, hidden), BF16),
            pltpu.SemaphoreType.DMA((16,)),
        ]
        if not first:
            scratch.append(pltpu.VMEM((count, width, channels), BF16))
            if has_flux:
                scratch.append(pltpu.VMEM(piece(count), BF16))
        return pl.pallas_call(
            functools.partial(side_kernel, (which, has_flux, split, first, len(prefetch))),
            out_shape=out_shape + [pltpu.VMEM(v.shape, v.dtype) for v in prefetch],
            in_specs=[VMEM] * len(close) + [smem] + [ANY] * len(prefetch),
            out_specs=[VMEM if first else ANY] * len(out_shape) + [VMEM] * len(prefetch),
            scratch_shapes=scratch,
            compiler_params=pltpu.CompilerParams(vmem_limit_bytes=LIMIT),
            cost_estimate=cost(count),
            name=f"side{which}_{int(first)}",
        )(*[near(v) for v in close], odd, *[far(v) for v in prefetch])

    held_shape = [pltpu.VMEM((PAD + middle, width, channels), BF16)]
    out_shape = [jax.ShapeDtypeStruct((rows, width, channels), BF16)]
    if has_flux:
        held_shape.append(pltpu.VMEM(piece(PAD + middle), BF16))
        out_shape.append(jax.ShapeDtypeStruct(piece(rows), BF16))
    held = side(True, one, [], held_shape, ())
    return side(False, two, list(held), out_shape, prefetch)


def stage_kernel(number, x_hbm, odd_ref, *refs):
    sources, (x_ref, one_ref, two_ref), targets, sem = refs[:number], refs[number : number + 3], refs[number + 3 : -1], refs[-1]
    last = x_hbm.shape[0] - PAD
    odd = odd_ref[0]
    pairs = [
        (x_hbm.at[pl.ds(odd * last, PAD)], two_ref),
        (x_hbm.at[pl.ds((1 - odd) * last, PAD)], one_ref),
        (x_hbm, x_ref),
        *zip(sources, targets),
    ]
    copies = [pltpu.make_async_copy(a, b, sem.at[n]) for n, (a, b) in enumerate(pairs)]
    for copy in copies:
        copy.start()
    for copy in copies:
        copy.wait()


def stage(x, odd, small):
    edge = pltpu.VMEM((PAD,) + x.shape[1:], x.dtype)
    return pl.pallas_call(
        functools.partial(stage_kernel, len(small)),
        out_shape=[pltpu.VMEM(x.shape, x.dtype), edge, edge] + [pltpu.VMEM(v.shape, v.dtype) for v in small],
        in_specs=[ANY, pl.BlockSpec(memory_space=pltpu.SMEM)] + [ANY] * len(small),
        out_specs=[VMEM] * (3 + len(small)),
        scratch_shapes=[pltpu.SemaphoreType.DMA((3 + len(small),))],
        compiler_params=pltpu.CompilerParams(vmem_limit_bytes=1 << 20),
        name="stage",
    )(far(x), odd, *[far(v) for v in small])


def ocean_in_kernel(split, ocean_ref, moved_ref, mask_ref, fi_ref, odd_ref, out_ref, edges_ref):
    rows, width, channels = out_ref.shape
    mask = jnp.transpose(mask_ref[...].astype(F32))
    order = list(range(PAD)) + list(range(rows - PAD, rows)) + list(range(PAD, rows - PAD))
    for i in order:
        moved = moved_ref[:, i].reshape(width, fi_ref.shape[0]) if split else moved_ref[i]
        forcing = jnp.dot(moved, fi_ref[...], preferred_element_type=F32)
        value = (ocean_ref[i].astype(F32) + mask[:, i : i + 1] * forcing).astype(BF16)
        out_ref[i] = value
        if i < PAD:
            edges_ref[1 - odd_ref[0], i] = value
        if i >= rows - PAD:
            edges_ref[odd_ref[0], i - rows + PAD] = value


def ocean_input(ocean, moved, mask, flux_in, odd, split):
    rows, width, channels = ocean.shape
    return pl.pallas_call(
        functools.partial(ocean_in_kernel, split),
        out_shape=[pltpu.VMEM((rows, width, channels), BF16), pltpu.VMEM((2, PAD, width, channels), BF16)],
        in_specs=[VMEM] * 4 + [pl.BlockSpec(memory_space=pltpu.SMEM)],
        out_specs=[VMEM] * 2,
        compiler_params=pltpu.CompilerParams(vmem_limit_bytes=8 << 20),
        cost_estimate=pl.CostEstimate(
            flops=2 * rows * width * channels * flux_in.shape[0], bytes_accessed=8 * rows * width * channels, transcendentals=0
        ),
        name="ocean_in",
    )(near(ocean), near(moved), near(mask), near(flux_in), odd)


def halos(one, two):
    size = lax.axis_size("band")
    inner = [(i, i ^ 1) for i in range(size)]
    outer = [(i, i + 1) for i in range(1, size - 1, 2)] + [(i + 1, i) for i in range(1, size - 1, 2)]
    return lax.ppermute(one, "band", inner), lax.ppermute(two, "band", outer)


def per_device(
    atm_state,
    ocean_state,
    dw_kernel,
    norm_gain,
    w_up,
    b_up,
    w_down,
    flux_out,
    flux_in,
    partner,
    remap,
    land_mask,
):
    height, width, channels = atm_state.shape
    size = lax.axis_size("band")
    share = width // size
    split = size if share % SUB == 0 else 0
    band_rows = remap.shape[0] // partner.shape[0]
    indices = jnp.repeat(partner, band_rows) * band_rows + remap
    shared = (w_up, w_down)

    odd = (lax.axis_index("band") % 2).astype(jnp.int32).reshape(1)

    atm, one, two, *small = stage(atm_state, odd, [dw_kernel.transpose(1, 2, 0, 3), norm_gain, b_up])
    halo = (*halos(one, two), odd)
    atm_next, surface, ocean, mask, fi = mix(
        0, atm, halo, shared, small, flux_out, split, (ocean_state, land_mask, flux_in)
    )
    if not split:
        surface = surface.reshape(height, size, share, -1).transpose(1, 0, 2, 3)
    spread = lax.all_to_all(surface, "band", split_axis=0, concat_axis=0, tiled=True)
    picked = jnp.take(spread.reshape((size * height,) + spread.shape[2:]), indices, axis=0, mode="clip")
    moved = lax.all_to_all(picked.reshape(spread.shape), "band", split_axis=0, concat_axis=0, tiled=True)
    if not split:
        moved = moved.transpose(1, 0, 2, 3).reshape(height, width, -1)
    ocean_in, edges = ocean_input(ocean, moved, mask, fi, odd, split)
    halo = (*halos(edges[0], edges[1]), odd)
    (ocean_next,) = mix(1, ocean_in, halo, shared, small)
    return (atm_next, ocean_next)


def solution(mesh):
    in_specs = (
        P(("ens", "band"), None, None),
        P(("ens", "band"), None, None),
        P(),
        P(),
        P(),
        P(),
        P(),
        P(),
        P(),
        P("ens"),
        P("ens"),
        P(("ens", "band"), None),
    )
    out_specs = (P(("ens", "band"), None, None), P(("ens", "band"), None, None))
    return jax.shard_map(
        per_device, mesh=mesh, in_specs=in_specs, out_specs=out_specs, check_vma=False
    )
```

time: 112 us -> 71.7 us (0.64)
  other arithmetic: 30.1 us -> 0.01 us
  Pallas kernels: 0 us -> 23.9 us
  waiting for transfers between devices: 38.5 us -> 15.1 us
  blocking collectives: 0 us -> 18.2 us
  matrix products: 11.2 us -> 0 us
  starting transfers between devices: 20.8 us -> 12 us
  local copies, waits for them, and re-layouts: 8.78 us -> 0.87 us
    reduce_sum x4 -> x0, other arithmetic: 27.7 us -> none  [the longest x2 23.9 us: conv_norm(): center = jnp.mean(total, axis=-1, keepdims=True)]
    pallas_call x0 -> x8, Pallas kernels: none -> 23.9 us  [the longest x4 14.5 us: side(): pl.pallas_call(functools.partial(side_kernel, (which, has_flux, split, fi...]
    all_to_all x0 -> x1, blocking collectives: none -> 18.2 us  [per_device(): lax.all_to_all(picked.reshape(spread.shape), 'band', split_axis=0, concat...]
    all_to_all x2 -> x1, waiting for transfers between devices: 28 us -> 13.9 us  [per_device(): lax.all_to_all(surface, 'band', split_axis=0, concat_axis=0, tiled=True)]
    dot_general x6 -> x0, matrix products: 11.2 us -> none  [the longest x2 5.77 us: mixer(): jnp.dot(normed, w_up[which], preferred_element_type=jnp.float32)]
    ppermute x4, waiting for transfers between devices: 10.5 us -> 1.2 us  [halos(): return (lax.ppermute(one, 'band', inner), lax.ppermute(two, 'band', outer))]
    all_to_all x2 -> x1, starting transfers between devices: 10.6 us -> 5.08 us  [per_device(): lax.all_to_all(surface, 'band', split_axis=0, concat_axis=0, tiled=True)]
    unnamed x40 -> x4, local copies, waits for them, and re-layouts: 3.71 us -> 0.01 us
  transfers between devices with their start and end apart: 6 -> 5, of which waited for: 5 -> 3; matrix products, arithmetic and copies ran while one was open for 2% -> 0% of each run, Pallas kernels for 0% -> 21%
where the time goes in v2:
time: 71.7 us; the launch traced here: 71.1 us
  Pallas kernels  23.9 us (33%)
  blocking collectives  18.2 us (25%)
  waiting for transfers between devices  15.1 us (21%)
  starting transfers between devices  12 us (17%)
  between operations  0.95 us (1%)
  local copies, waits for them, and re-layouts  0.87 us (1%)
    all_to_all x1, blocking collectives, per_device(): lax.all_to_all(picked.reshape(spread.shape), 'band', split_axis=0, concat...  18.2 us
    pallas_call x4, Pallas kernels, side(): pl.pallas_call(functools.partial(side_kernel, (which, has_flux, split, fi...  14.5 us
    all_to_all x1, waiting for transfers between devices, per_device(): lax.all_to_all(surface, 'band', split_axis=0, concat_axis=0, tiled=True)  13.9 us
    pallas_call x2, Pallas kernels, mix(): pl.pallas_call(functools.partial(own_kernel, which), out_shape=[pltpu.VME...  7.47 us
    ppermute x4, starting transfers between devices, halos(): return (lax.ppermute(one, 'band', inner), lax.ppermute(two, 'band', outer))  6.96 us
    all_to_all x1, starting transfers between devices, per_device(): lax.all_to_all(surface, 'band', split_axis=0, concat_axis=0, tiled=True)  5.08 us
  transfers between devices with their start and end apart: 5, of which 3 were waited for; matrix products, arithmetic and copies ran while one was open for 0% of the time, Pallas kernels for 21%

profile of v2, /device:TPU:9, one launch (start us, length us, event | category | flops | bytes accessed | tf_op | source)
XLA Modules:
  0.0 71.1 jit_solution(9301117200834891272)
XLA Ops:
  0.6 1.4 %stage.1 = (bf16[8,128,384]{2,1,0:T(8,128)(2,1)S(1)}, bf16[3,128,384]{2,1,0:T(8,128)(2,1)S(1)}, bf16[3,128,384]{2,1,0:T(8,128)(2,1)S(1)}, f32[7,7,2,384]{3,2,1,0...) custom-call(bf16[8,128,384]{2,1,0:T(8,128)(2,1)} %x_hbm.1, s32[1]{0:T(128)} %bitcast.odd_ref.refs_9_.refs_11_.refs_8_, ...), custom_call_target="tpu_custom_call" | custom-call | tf_op jit(solution)/shard_map/stage/pallas_call | solution.py:397
  2.0 0.7 %collective-permute-start.1 = (bf16[3,128,384]{2,1,0:T(8,128)(2,1)S(1)}, bf16[3,128,384]{2,1,0:T(8,128)(2,1)S(1)}, u32[]{:S(2)}, u32[]{:S(2)}) collective-permute-start(bf16[3,128,384]{2,1,0:T(8,128)(2,1)S(1)} %get-tuple-element.33), channel_id=1, source_target_pairs={{0,1},{1,0},{2,3},{3,2},{4,5},{5,4},{6,7},{7,6},{8,9},{9,8},{10,11... | collective-permute-start | bytes 884744 | tf_op jit(solution)/shard_map/ppermute | solution.py:442
  2.8 3.0 %collective-permute-start = (bf16[3,128,384]{2,1,0:T(8,128)(2,1)S(1)}, bf16[3,128,384]{2,1,0:T(8,128)(2,1)S(1)}, u32[]{:S(2)}, u32[]{:S(2)}) collective-permute-start(bf16[3,128,384]{2,1,0:T(8,128)(2,1)S(1)} %get-tuple-element.31), channel_id=1, source_target_pairs={{1,2},{3,4},{5,6},{7,8},{9,10},{11,12},{13,14},{2,1},{4,3},{6,5},{... | collective-permute-start | bytes 884744 | tf_op jit(solution)/shard_map/ppermute | solution.py:442
  5.8 3.7 %own0.1 = (f32[8,128,384]{2,1,0:T(8,128)S(1)}, bf16[384,1536]{1,0:T(8,128)(2,1)S(1)}, bf16[384,1536]{1,0:T(8,128)(2,1)S(1)}, bf16[384,256]{1,0:T(8,128)(2,1)S(1)}) custom-call(bf16[8,128,384]{2,1,0:T(8,128)(2,1)S(1)} %get-tuple-element.24.refs_0_, f32[7,7,2,384]{3,2,1,0:T(2,128)S(1)} %get-tuple-element.25.refs_1_.refs_4_, bf16[2,384,1536]{2,1,0:T(8,128)(2,1)} %refs_2_.5, ...), custom_call_target="tpu_custom_call" | custom-call | flops 23592960 | bytes 3145728 | tf_op jit(solution)/shard_map/own0/pallas_call | solution.py:327
  9.6 0.0 collective-permute-done.1.refs_7_
  9.6 3.9 %side0_1.1 = (bf16[5,128,384]{2,1,0:T(8,128)(2,1)S(1)}, bf16[16,5,8,256]{3,2,1,0:T(8,128)(2,1)S(1)}) custom-call(bf16[8,128,384]{2,1,0:T(8,128)(2,1)S(1)} %get-tuple-element.24.refs_0_, f32[8,128,384]{2,1,0:T(8,128)S(1)} %get-tuple-element.26.refs_1_, bf16[384,1536]{1,0:T(8,128)(2,1)S(1)} %get-tuple-element.27.refs_2_, ...), custom_call_target="tpu_custom_call" | custom-call | flops 1509949440 | bytes 3440640 | tf_op jit(solution)/shard_map/side0_1/pallas_call | solution.py:358
  13.5 0.5 collective-permute-done.refs_7_
  14.0 3.6 %side0_0.1 = (bf16[8,128,384]{2,1,0:T(8,128)(2,1)}, bf16[16,8,8,256]{3,2,1,0:T(8,128)(2,1)}, bf16[8,128,384]{2,1,0:T(8,128)(2,1)S(1)}, s32[8,128]{1,0:T(8,128)S(1)}, bf16[256,384]{1,0:T(8,128)(2,1)S(1)}) custom-call(bf16[8,128,384]{2,1,0:T(8,128)(2,1)S(1)} %get-tuple-element.24.refs_0_, f32[8,128,384]{2,1,0:T(8,128)S(1)} %get-tuple-element.26.refs_1_, ...), custom_call_target="tpu_custom_call" | custom-call | flops 905969664 | bytes 2064384 | tf_op jit(solution)/shard_map/side0_0/pallas_call | solution.py:358
  17.5 5.1 %all-to-all-start = ((bf16[16,8,8,256]{3,2,1,0:T(8,128)(2,1)}), bf16[16,8,8,256]{3,2,1,0:T(8,128)(2,1)S(1)}, u32[]{:S(2)}, u32[]{:S(2)}) async-start(bf16[16,8,8,256]{3,2,1,0:T(8,128)(2,1)} %get-tuple-element.38), calls=%async_computation | async-start | bytes 1048576 | tf_op jit(solution)/shard_map/all_to_all | solution.py:476
  22.6 0.0 copy-done
  22.6 0.1 broadcast_in_dim.7
  22.7 0.1 mul.12
  22.8 13.9 %all-to-all-done = bf16[16,8,8,256]{3,2,1,0:T(8,128)(2,1)S(1)} async-done(((bf16[16,8,8,256]{3,2,1,0:T(8,128)(2,1)}), bf16[16,8,8,256]{3,2,1,0:T(8,128)(2,1)S(1)}, u32[]{:S(2)}, u32[]{:S(2)}) %all-to-all-start) | async-done | bytes 524320 | tf_op jit(solution)/shard_map/all_to_all | solution.py:476
  36.7 0.6 gather_fusion
  37.4 18.2 %all_to_all.10.moved_ref = bf16[16,8,8,256]{3,2,1,0:T(8,128)(2,1)S(1)} all-to-all(bf16[16,8,8,256]{3,2,1,0:T(8,128)(2,1)S(1)} %bitcast.9), channel_id=1, replica_groups=mesh['ens'=2,'band'=16] {'band'}, dimensions={0} | all-to-all | bytes 1048576 | tf_op jit(solution)/shard_map/all_to_all | solution.py:478
  55.6 0.5 ocean_in.1
  56.1 0.1 slice_bitcast_fusion
  56.2 0.1 collective-permute-start.3
  56.3 3.1 %collective-permute-start.2 = (bf16[3,128,384]{2,1,0:T(8,128)(2,1)S(1)}, bf16[3,128,384]{2,1,0:T(8,128)(2,1)S(1)}, u32[]{:S(2)}, u32[]{:S(2)}) collective-permute-start(bf16[3,128,384]{2,1,0:T(8,128)(2,1)S(1)} %get-tuple-element.47), channel_id=1, source_target_pairs={{1,2},{3,4},{5,6},{7,8},{9,10},{11,12},{13,14},{2,1},{4,3},{6,5},{... | collective-permute-start | bytes 884744 | tf_op jit(solution)/shard_map/ppermute | solution.py:442
  59.4 3.7 %own1.1 = (f32[8,128,384]{2,1,0:T(8,128)S(1)}, bf16[384,1536]{1,0:T(8,128)(2,1)S(1)}, bf16[384,1536]{1,0:T(8,128)(2,1)S(1)}) custom-call(bf16[8,128,384]{2,1,0:T(8,128)(2,1)S(1)} %get-tuple-element.41.refs_0_, f32[7,7,2,384]{3,2,1,0:T(2,128)S(1)} %get-tuple-element.25.refs_1_.refs_4_, bf16[2,384,1536]{2,1,0:T(8,128)(2,1)} %refs_2_.5, ...), custom_call_target="tpu_custom_call" | custom-call | flops 23592960 | bytes 3145728 | tf_op jit(solution)/shard_map/own1/pallas_call | solution.py:327
  63.1 0.0 collective-permute-done.3.refs_7_
  63.1 3.6 %side1_1.1.refs_8_ = bf16[5,128,384]{2,1,0:T(8,128)(2,1)S(1)} custom-call(bf16[8,128,384]{2,1,0:T(8,128)(2,1)S(1)} %get-tuple-element.41.refs_0_, f32[8,128,384]{2,1,0:T(8,128)S(1)} %get-tuple-element.42.refs_1_, bf16[384,1536]{1,0:T(8,128)(2,1)S(1)} %get-tuple-element.43.refs_2_, bf16[384,1536]{1,0:T(8,128)(2,1)S(1)} %get-tuple-element.44.refs_3_, ...), custom_call_target="tpu_custom_call" | custom-call | flops 1509949440 | bytes 3440640 | tf_op jit(solution)/shard_map/side1_1/pallas_call | solution.py:358
  66.7 0.7 %collective-permute-done.2.refs_7_ = bf16[3,128,384]{2,1,0:T(8,128)(2,1)S(1)} collective-permute-done((bf16[3,128,384]{2,1,0:T(8,128)(2,1)S(1)}, bf16[3,128,384]{2,1,0:T(8,128)(2,1)S(1)}, u32[]{:S(2)}, u32[]{:S(2)}) %collective-permute-start.2) | collective-permute-done | bytes 294944 | tf_op jit(solution)/shard_map/ppermute | solution.py:442
  67.5 3.5 %side1_0.1 = bf16[8,128,384]{2,1,0:T(8,128)(2,1)} custom-call(bf16[8,128,384]{2,1,0:T(8,128)(2,1)S(1)} %get-tuple-element.41.refs_0_, f32[8,128,384]{2,1,0:T(8,128)S(1)} %get-tuple-element.42.refs_1_, bf16[384,1536]{1,0:T(8,128)(2,1)S(1)} %get-tuple-element.43.refs_2_, bf16[384,1536]{1,0:T(8,128)(2,1)S(1)} %get-tuple-element.44.refs_3_, ...), custom_call_target="tpu_custom_call" | custom-call | flops 905969664 | bytes 2064384 | tf_op jit(solution)/shard_map/side1_0/pallas_call | solution.py:358
  (6 shorter events, 0.0 us)
Async XLA Ops:
  2.0 7.5 %collective-permute-start.1 = (bf16[3,128,384]{2,1,0:T(8,128)(2,1)S(1)}, bf16[3,128,384]{2,1,0:T(8,128)(2,1)S(1)}, u32[]{:S(2)}, u32[]{:S(2)}) collective-permute-start(bf16[3,128,384]{2,1,0:T(8,128)(2,1)S(1)} %get-tuple-element.33), channel_id=1, source_target_pairs={{0,1},{1,0},{2,3},{3,2},{4,5},{5,4},{6,7},{7,6},{8,9},{9,8},{10,11... | collective-permute-start | bytes 884744 | tf_op jit(solution)/shard_map/ppermute | solution.py:442
  2.8 11.2 %collective-permute-start = (bf16[3,128,384]{2,1,0:T(8,128)(2,1)S(1)}, bf16[3,128,384]{2,1,0:T(8,128)(2,1)S(1)}, u32[]{:S(2)}, u32[]{:S(2)}) collective-permute-start(bf16[3,128,384]{2,1,0:T(8,128)(2,1)S(1)} %get-tuple-element.31), channel_id=1, source_target_pairs={{1,2},{3,4},{5,6},{7,8},{9,10},{11,12},{13,14},{2,1},{4,3},{6,5},{... | collective-permute-start | bytes 884744 | tf_op jit(solution)/shard_map/ppermute | solution.py:442
  14.0 8.6 %copy-start = (s32[16]{0:T(128)S(1)}, s32[16]{0:T(128)}, u32[]{:S(2)}) copy-start(s32[16]{0:T(128)} %param.21) | copy-start | bytes 196
  14.0 8.8 %copy-start.1 = (s32[128]{0:T(128)S(1)}, s32[128]{0:T(128)}, u32[]{:S(2)}) copy-start(s32[128]{0:T(128)} %param.22) | copy-start | bytes 1540
  17.5 19.2 %all-to-all-start = ((bf16[16,8,8,256]{3,2,1,0:T(8,128)(2,1)}), bf16[16,8,8,256]{3,2,1,0:T(8,128)(2,1)S(1)}, u32[]{:S(2)}, u32[]{:S(2)}) async-start(bf16[16,8,8,256]{3,2,1,0:T(8,128)(2,1)} %get-tuple-element.38), calls=%async_computation | async-start | bytes 1048576 | tf_op jit(solution)/shard_map/all_to_all | solution.py:476
  56.2 6.9 %collective-permute-start.3 = (bf16[3,128,384]{2,1,0:T(8,128)(2,1)S(1)}, bf16[3,128,384]{2,1,0:T(8,128)(2,1)S(1)}, u32[]{:S(2)}, u32[]{:S(2)}) collective-permute-start(bf16[3,128,384]{2,1,0:T(8,128)(2,1)S(1)} %get-tuple-element.46), channel_id=1, source_target_pairs={{0,1},{1,0},{2,3},{3,2},{4,5},{5,4},{6,7},{7,6},{8,9},{9,8},{10,11... | collective-permute-start | bytes 884744 | tf_op jit(solution)/shard_map/ppermute | solution.py:442
  56.3 11.2 %collective-permute-start.2 = (bf16[3,128,384]{2,1,0:T(8,128)(2,1)S(1)}, bf16[3,128,384]{2,1,0:T(8,128)(2,1)S(1)}, u32[]{:S(2)}, u32[]{:S(2)}) collective-permute-start(bf16[3,128,384]{2,1,0:T(8,128)(2,1)S(1)} %get-tuple-element.47), channel_id=1, source_target_pairs={{1,2},{3,4},{5,6},{7,8},{9,10},{11,12},{13,14},{2,1},{4,3},{6,5},{... | collective-permute-start | bytes 884744 | tf_op jit(solution)/shard_map/ppermute | solution.py:442

commit v3 on v2

--- a/solution.py
+++ b/solution.py
@@ -6,6 +6,7 @@
 from jax.experimental import pallas as pl
 from jax.experimental.pallas import tpu as pltpu
 from jax.sharding import PartitionSpec as P
+
 
 LANES = 128
 SUB = 8
@@ -17,6 +18,10 @@
 VMEM = pl.BlockSpec(memory_space=pltpu.VMEM)
 ANY = pl.BlockSpec(memory_space=pl.ANY)
 LIMIT = 24 << 20
+
+
+def parity():
+    return lax.axis_index("band") % 2
 
 
 def far(x):
@@ -75,7 +80,7 @@
         return outs
 
 
-def fill(load, rows, products, derived, width, lane_blocks):
+def fill(load, rows, derived, width, lane_blocks):
     last = width // SUB - 1
     for block in range(width // SUB):
         for cb in range(lane_blocks):
@@ -150,13 +155,15 @@
         hidden[:, cols] = gelu(u + bu[which : which + 1, cols]).astype(BF16)
 
 
-def contract(split, base, hidden, x_ref, wd, out, flux_refs):
+def contract(split, base, hidden, x_ref, wd, out, begin, size, flux_refs):
     count, width, channels = out.shape
+    cols = slice(begin, begin + size)
     update = lax.dot_general(
-        hidden[...], wd[...], (((1,), (1,)), ((), ())), preferred_element_type=F32
+        hidden[...], wd[cols, :], (((1,), (1,)), ((), ())), preferred_element_type=F32
     )
     for n in range(count):
-        out[n] = (x_ref[base + n].astype(F32) + update[n * width : (n + 1) * width]).astype(BF16)
+        state = x_ref[base + n, :, cols].astype(F32)
+        out[n, :, cols] = (state + update[n * width : (n + 1) * width]).astype(BF16)
     if flux_refs:
         fo, surf = flux_refs
         flux = jnp.dot(out[...].reshape(count * width, channels), fo[...], preferred_element_type=F32).astype(BF16)
@@ -181,14 +188,12 @@
     lane_blocks = channels // LANES
     plan = Plan(rows, TAPS)
     copies = [
-        pltpu.make_async_copy(source.at[which] if len(source.shape) == 3 else source, target, sem.at[n])
+        pltpu.make_async_copy(source.at[which] if len(source.shape) > len(target.shape) else source, target, sem.at[n])
         for n, (source, target) in enumerate(zip(sources, targets))
     ]
     for copy in copies:
         copy.start()
-    fill(
-        lambda m, lons, lanes: x_ref[m, lons, lanes], own_rows(plan), plan.leaves, derived, width, lane_blocks
-    )
+    fill(lambda m, lons, lanes: x_ref[m, lons, lanes], own_rows(plan), derived, width, lane_blocks)
     tap_rows(kernel, which, plan, weights)
     wide = 2 if width % (2 * SUB) == 0 else 1
     for cb in range(lane_blocks):
@@ -224,7 +229,6 @@
     rows, width, channels = x_ref.shape
     middle = rows - 2 * PAD
     held = [refs.pop(0) for _ in range((1 + has_flux) * (not first))]
-    odd_ref = refs.pop(0)
     sources = [refs.pop(0) for _ in range(prefetch)]
     surf = None
     if first:
@@ -233,22 +237,23 @@
         targets = [refs.pop(0) for _ in range(prefetch)]
         derived, weights, conv, hidden, sem = refs
     else:
-        out_hbm = refs.pop(0)
-        surf_hbm = refs.pop(0) if has_flux else None
+        out_all = refs.pop(0)
+        surf_all = refs.pop(0) if has_flux else None
         targets = [refs.pop(0) for _ in range(prefetch)]
-        derived, weights, conv, hidden, sem, out = refs[:6]
-        surf = refs[6] if has_flux else None
+        derived, weights, conv, hidden, sem, out = refs if not has_flux else (*refs, None)
     lane_blocks = channels // LANES
-    before = odd_ref[0] if first else 1 - odd_ref[0]
+    before = parity() if first else 1 - parity()
     count = PAD + middle if first else PAD
     base = (1 - before) * (rows - count)
 
     copies = [(source, target) for source, target in zip(sources, targets)]
     if not first:
         place = before * PAD
-        copies.append((held[0], out_hbm.at[pl.ds(place, PAD + middle)]))
+        copies.append((held[0], out_all.at[pl.ds(place, PAD + middle)]))
         if has_flux:
-            copies.append((held[1], surface_rows(split, surf_hbm, place, PAD + middle)))
+            out = out_all.at[pl.ds(base, PAD)]
+            copies.append((held[1], surface_rows(split, surf_all, place, PAD + middle)))
+            surf = surface_rows(split, surf_all, base, PAD)
     copies = [pltpu.make_async_copy(a, b, sem.at[n]) for n, (a, b) in enumerate(copies)]
     for copy in copies:
         copy.start()
@@ -260,7 +265,7 @@
     def taps(j):
         return kernel[before * (PAD - 1 - j) + (1 - before) * (PAD + 1 + j), :, which, :]
 
-    fill(lambda m, lons, lanes: halo_ref[m, lons, lanes], rows_of, EDGE_PRODUCTS, derived, width, lane_blocks)
+    fill(lambda m, lons, lanes: halo_ref[m, lons, lanes], rows_of, derived, width, lane_blocks)
     for n, (_, add, subtract) in enumerate(EDGE_PRODUCTS):
         weights[n, 0:TAPS, :] = taps(add) if subtract is None else taps(add) - taps(subtract)
     wide = 2 if width % (2 * SUB) == 0 else 1
@@ -285,28 +290,32 @@
         for n in range(middle):
             conv[before * PAD + n] = acc_ref[PAD + n]
     expand(which, conv[...].reshape(count * width, channels), gain, wu, bu, hidden)
-    contract(split, base, hidden, x_ref, wd, out, (fo, surf) if has_flux else None)
-    if not first:
-        pairs = [(out, out_hbm.at[pl.ds(base, PAD)])]
-        if has_flux:
-            pairs.append((surf, surface_rows(split, surf_hbm, base, PAD)))
-        for a, b in pairs:
-            copies.append(pltpu.make_async_copy(a, b, sem.at[len(copies)]))
+    if has_flux or first:
+        contract(split, base, hidden, x_ref, wd, out, 0, channels, (fo, surf) if has_flux else None)
+    else:
+        for begin in range(0, channels, TILE):
+            size = min(TILE, channels - begin)
+            contract(split, base, hidden, x_ref, wd, out, begin, size, None)
+            cols = pl.ds(begin, size)
+            copies.append(
+                pltpu.make_async_copy(
+                    out.at[:, :, cols], out_all.at[pl.ds(base, PAD), :, cols], sem.at[len(copies)]
+                )
+            )
             copies[-1].start()
     for copy in copies:
         copy.wait()
 
 
-def mix(which, x, halo, shared, small, flux_out=None, split=0, prefetch=()):
+def mix(which, x, halo, shared, small, flux_out=None, split=0, prefetch=(), flush=None):
     w_up, w_down = shared
     kernel, gain, b_up = small
-    one, two, odd = halo
+    one, two = halo
     rows, width, channels = x.shape
     has_flux = flux_out is not None
     hidden = w_up.shape[-1]
     blocks = channels // LANES
     middle = rows - 2 * PAD
-    smem = pl.BlockSpec(memory_space=pltpu.SMEM)
 
     def piece(count):
         return (split, count, width // split, depth) if split else (count, width, depth)
@@ -324,11 +333,19 @@
         model.append(flux_out)
         loaded.append(pltpu.VMEM(flux_out.shape, BF16))
     leaves = len(Plan(rows, TAPS).leaves)
+    out_specs = [VMEM] * (1 + len(loaded))
+    in_specs = [VMEM] * 2 + [ANY] * len(model)
+    model = [far(v) for v in model]
+    if flush is not None:
+        model.append(near(flush))
+        in_specs.append(VMEM)
+        loaded.append(jax.ShapeDtypeStruct(flush.shape, flush.dtype))
+        out_specs.append(ANY)
     acc, *loaded = pl.pallas_call(
         functools.partial(own_kernel, which),
         out_shape=[pltpu.VMEM((rows, width, channels), F32)] + loaded,
-        in_specs=[VMEM] * 2 + [ANY] * len(model),
-        out_specs=[VMEM] * (1 + len(loaded)),
+        in_specs=in_specs,
+        out_specs=out_specs,
         scratch_shapes=[
             pltpu.VMEM((blocks, leaves, width + 2 * SUB, LANES), F32),
             pltpu.VMEM((leaves, SUB, channels), F32),
@@ -338,8 +355,8 @@
         cost_estimate=pl.CostEstimate(
             flops=60 * rows * width * channels, bytes_accessed=8 * rows * width * channels, transcendentals=0
         ),
-        name=f"own{which}",
-    )(near(x), near(kernel), *[far(v) for v in model])
+    )(near(x), near(kernel), *model)
+    flushed = [loaded.pop()] if flush is not None else []
 
     def side(first, halo_rows, held, out_shape, prefetch):
         count = PAD + middle if first else PAD
@@ -352,33 +369,31 @@
             pltpu.SemaphoreType.DMA((16,)),
         ]
         if not first:
-            scratch.append(pltpu.VMEM((count, width, channels), BF16))
-            if has_flux:
-                scratch.append(pltpu.VMEM(piece(count), BF16))
+            scratch += [] if has_flux else [pltpu.VMEM((count, width, channels), BF16)]
         return pl.pallas_call(
             functools.partial(side_kernel, (which, has_flux, split, first, len(prefetch))),
             out_shape=out_shape + [pltpu.VMEM(v.shape, v.dtype) for v in prefetch],
-            in_specs=[VMEM] * len(close) + [smem] + [ANY] * len(prefetch),
-            out_specs=[VMEM if first else ANY] * len(out_shape) + [VMEM] * len(prefetch),
+            in_specs=[VMEM] * len(close) + [ANY] * len(prefetch),
+            out_specs=[VMEM if first or has_flux else ANY] + [VMEM] * (len(out_shape) - 1 + len(prefetch)),
             scratch_shapes=scratch,
             compiler_params=pltpu.CompilerParams(vmem_limit_bytes=LIMIT),
             cost_estimate=cost(count),
-            name=f"side{which}_{int(first)}",
-        )(*[near(v) for v in close], odd, *[far(v) for v in prefetch])
+        )(*[near(v) for v in close], *[far(v) for v in prefetch])
 
     held_shape = [pltpu.VMEM((PAD + middle, width, channels), BF16)]
-    out_shape = [jax.ShapeDtypeStruct((rows, width, channels), BF16)]
+    full = pltpu.VMEM if has_flux else jax.ShapeDtypeStruct
+    out_shape = [full((rows, width, channels), BF16)]
     if has_flux:
         held_shape.append(pltpu.VMEM(piece(PAD + middle), BF16))
-        out_shape.append(jax.ShapeDtypeStruct(piece(rows), BF16))
+        out_shape.append(pltpu.VMEM(piece(rows), BF16))
     held = side(True, one, [], held_shape, ())
-    return side(False, two, list(held), out_shape, prefetch)
-
-
-def stage_kernel(number, x_hbm, odd_ref, *refs):
+    return [*side(False, two, list(held), out_shape, prefetch), *flushed]
+
+
+def stage_kernel(number, x_hbm, *refs):
     sources, (x_ref, one_ref, two_ref), targets, sem = refs[:number], refs[number : number + 3], refs[number + 3 : -1], refs[-1]
     last = x_hbm.shape[0] - PAD
-    odd = odd_ref[0]
+    odd = parity()
     pairs = [
         (x_hbm.at[pl.ds(odd * last, PAD)], two_ref),
         (x_hbm.at[pl.ds((1 - odd) * last, PAD)], one_ref),
@@ -392,21 +407,45 @@
         copy.wait()
 
 
-def stage(x, odd, small):
+def stage(x, small):
     edge = pltpu.VMEM((PAD,) + x.shape[1:], x.dtype)
     return pl.pallas_call(
         functools.partial(stage_kernel, len(small)),
         out_shape=[pltpu.VMEM(x.shape, x.dtype), edge, edge] + [pltpu.VMEM(v.shape, v.dtype) for v in small],
-        in_specs=[ANY, pl.BlockSpec(memory_space=pltpu.SMEM)] + [ANY] * len(small),
+        in_specs=[ANY] * (1 + len(small)),
         out_specs=[VMEM] * (3 + len(small)),
         scratch_shapes=[pltpu.SemaphoreType.DMA((3 + len(small),))],
         compiler_params=pltpu.CompilerParams(vmem_limit_bytes=1 << 20),
         name="stage",
-    )(far(x), odd, *[far(v) for v in small])
-
-
-def ocean_in_kernel(split, ocean_ref, moved_ref, mask_ref, fi_ref, odd_ref, out_ref, edges_ref):
-    rows, width, channels = out_ref.shape
+    )(far(x), *[far(v) for v in small])
+
+
+def pick_kernel(partner_ref, remap_ref, x_ref, out_ref):
+    bands, rows = out_ref.shape[:2]
+    for o in range(bands):
+        for r in range(rows):
+            out_ref[o, r] = x_ref[partner_ref[o], remap_ref[o * rows + r]]
+
+
+def pick_rows(x, partner, remap):
+    if x.shape[2] % SUB:
+        height = x.shape[1]
+        indices = jnp.repeat(partner, height) * height + remap
+        return jnp.take(x.reshape((-1,) + x.shape[2:]), indices, axis=0, mode="clip").reshape(x.shape)
+    smem = pl.BlockSpec(memory_space=pltpu.SMEM)
+    return pl.pallas_call(
+        pick_kernel,
+        out_shape=pltpu.VMEM(x.shape, x.dtype),
+        in_specs=[smem, smem, VMEM],
+        out_specs=VMEM,
+        compiler_params=pltpu.CompilerParams(vmem_limit_bytes=1 << 20),
+        name="pick",
+    )(*[pltpu.with_memory_space_constraint(v, pltpu.SMEM) for v in (partner, remap)], near(x))
+
+
+def ocean_in_kernel(split, ocean_ref, moved_ref, mask_ref, fi_ref, out_ref, edges_ref):
+    rows, width, _ = out_ref.shape
+    odd = parity()
     mask = jnp.transpose(mask_ref[...].astype(F32))
     order = list(range(PAD)) + list(range(rows - PAD, rows)) + list(range(PAD, rows - PAD))
     for i in order:
@@ -415,31 +454,33 @@
         value = (ocean_ref[i].astype(F32) + mask[:, i : i + 1] * forcing).astype(BF16)
         out_ref[i] = value
         if i < PAD:
-            edges_ref[1 - odd_ref[0], i] = value
+            edges_ref[1 - odd, i] = value
         if i >= rows - PAD:
-            edges_ref[odd_ref[0], i - rows + PAD] = value
-
-
-def ocean_input(ocean, moved, mask, flux_in, odd, split):
+            edges_ref[odd, i - rows + PAD] = value
+
+
+def ocean_input(ocean, moved, mask, flux_in, split):
     rows, width, channels = ocean.shape
     return pl.pallas_call(
         functools.partial(ocean_in_kernel, split),
         out_shape=[pltpu.VMEM((rows, width, channels), BF16), pltpu.VMEM((2, PAD, width, channels), BF16)],
-        in_specs=[VMEM] * 4 + [pl.BlockSpec(memory_space=pltpu.SMEM)],
+        in_specs=[VMEM] * 4,
         out_specs=[VMEM] * 2,
         compiler_params=pltpu.CompilerParams(vmem_limit_bytes=8 << 20),
         cost_estimate=pl.CostEstimate(
             flops=2 * rows * width * channels * flux_in.shape[0], bytes_accessed=8 * rows * width * channels, transcendentals=0
         ),
         name="ocean_in",
-    )(near(ocean), near(moved), near(mask), near(flux_in), odd)
+    )(near(ocean), near(moved), near(mask), near(flux_in))
 
 
 def halos(one, two):
     size = lax.axis_size("band")
     inner = [(i, i ^ 1) for i in range(size)]
     outer = [(i, i + 1) for i in range(1, size - 1, 2)] + [(i + 1, i) for i in range(1, size - 1, 2)]
-    return lax.ppermute(one, "band", inner), lax.ppermute(two, "band", outer)
+    two = lax.ppermute(two, "band", outer)
+    one = lax.ppermute(one, "band", inner)
+    return one, two
 
 
 def per_device(
@@ -456,31 +497,27 @@
     remap,
     land_mask,
 ):
-    height, width, channels = atm_state.shape
+    height, width, _ = atm_state.shape
     size = lax.axis_size("band")
     share = width // size
     split = size if share % SUB == 0 else 0
-    band_rows = remap.shape[0] // partner.shape[0]
-    indices = jnp.repeat(partner, band_rows) * band_rows + remap
     shared = (w_up, w_down)
 
-    odd = (lax.axis_index("band") % 2).astype(jnp.int32).reshape(1)
-
-    atm, one, two, *small = stage(atm_state, odd, [dw_kernel.transpose(1, 2, 0, 3), norm_gain, b_up])
-    halo = (*halos(one, two), odd)
+    atm, one, two, *small = stage(atm_state, [dw_kernel.transpose(1, 2, 0, 3), norm_gain, b_up])
+    halo = halos(one, two)
     atm_next, surface, ocean, mask, fi = mix(
         0, atm, halo, shared, small, flux_out, split, (ocean_state, land_mask, flux_in)
     )
     if not split:
         surface = surface.reshape(height, size, share, -1).transpose(1, 0, 2, 3)
     spread = lax.all_to_all(surface, "band", split_axis=0, concat_axis=0, tiled=True)
-    picked = jnp.take(spread.reshape((size * height,) + spread.shape[2:]), indices, axis=0, mode="clip")
-    moved = lax.all_to_all(picked.reshape(spread.shape), "band", split_axis=0, concat_axis=0, tiled=True)
+    picked = pick_rows(spread, partner, remap)
+    moved = lax.all_to_all(picked, "band", split_axis=0, concat_axis=0, tiled=True)
     if not split:
         moved = moved.transpose(1, 0, 2, 3).reshape(height, width, -1)
-    ocean_in, edges = ocean_input(ocean, moved, mask, fi, odd, split)
-    halo = (*halos(edges[0], edges[1]), odd)
-    (ocean_next,) = mix(1, ocean_in, halo, shared, small)
+    ocean_in, edges = ocean_input(ocean, moved, mask, fi, split)
+    halo = halos(edges[0], edges[1])
+    ocean_next, atm_next = mix(1, ocean_in, halo, shared, small, flush=atm_next)
     return (atm_next, ocean_next)
 
 
@@ -500,6 +537,5 @@
         P(("ens", "band"), None),
     )
     out_specs = (P(("ens", "band"), None, None), P(("ens", "band"), None, None))
-    return jax.shard_map(
-        per_device, mesh=mesh, in_specs=in_specs, out_specs=out_specs, check_vma=False
-    )
+
+    return jax.shard_map(per_device, mesh=mesh, in_specs=in_specs, out_specs=out_specs, check_vma=False)

time: 71.7 us -> 71.2 us (level)
  blocking collectives: 18.2 us -> 37.2 us
  waiting for transfers between devices: 15.1 us -> 1.1 us
  starting transfers between devices: 12 us -> 6.95 us
  local copies, waits for them, and re-layouts: 0.87 us -> 0.07 us
    all_to_all x1 -> x2, blocking collectives: 18.2 us -> 37.2 us  [the longest x1 19 us: per_device(): lax.all_to_all(surface, 'band', split_axis=0, concat_axis=0, tiled=True)]
    all_to_all x1 -> x0, waiting for transfers between devices: 13.9 us -> none  [per_device(): lax.all_to_all(surface, 'band', split_axis=0, concat_axis=0, tiled=True)]
    all_to_all x1 -> x0, starting transfers between devices: 5.08 us -> none  [per_device(): lax.all_to_all(surface, 'band', split_axis=0, concat_axis=0, tiled=True)]
    pallas_call x0 -> x1, Pallas kernels: none -> 0.72 us  [pick_rows(): pl.pallas_call(pick_kernel, out_shape=pltpu.VMEM(x.shape, x.dtype), in_sp...]
  transfers between devices with their start and end apart: 5 -> 4, of which waited for: 3 -> 2; matrix products, arithmetic and copies ran while one was open for 0% -> 0% of each run, Pallas kernels for 21% -> 21%
where the time goes in v3:
time: 71.2 us; the launch traced here: 70.7 us
  blocking collectives  37.2 us (52%)
  Pallas kernels  24.4 us (34%)
  starting transfers between devices  6.95 us (10%)
  waiting for transfers between devices  1.1 us (2%)
  between operations  0.91 us (1%)
    all_to_all x1, blocking collectives, per_device(): lax.all_to_all(surface, 'band', split_axis=0, concat_axis=0, tiled=True)  19 us
    all_to_all x1, blocking collectives, per_device(): lax.all_to_all(picked, 'band', split_axis=0, concat_axis=0, tiled=True)  18.2 us
    pallas_call x4, Pallas kernels, side(): pl.pallas_call(functools.partial(side_kernel, (which, has_flux, split, fi...  14.3 us
    pallas_call x2, Pallas kernels, mix(): pl.pallas_call(functools.partial(own_kernel, which), out_shape=[pltpu.VME...  7.47 us
    ppermute x2, starting transfers between devices, halos(): two = lax.ppermute(two, 'band', outer)  6.14 us
  transfers between devices with their start and end apart: 4, of which 2 were waited for; matrix products, arithmetic and copies ran while one was open for 0% of the time, Pallas kernels for 21%

profile of v3, /device:TPU:9, one launch (start us, length us, event | category | flops | bytes accessed | tf_op | source)
XLA Modules:
  0.0 70.7 jit_solution(15125924941952594374)
XLA Ops:
  0.6 1.4 %stage.1 = (bf16[8,128,384]{2,1,0:T(8,128)(2,1)S(1)}, bf16[3,128,384]{2,1,0:T(8,128)(2,1)S(1)}, bf16[3,128,384]{2,1,0:T(8,128)(2,1)S(1)}, f32[7,7,2,384]{3,2,1,0...) custom-call(bf16[8,128,384]{2,1,0:T(8,128)(2,1)} %x_hbm.1, f32[7,7,2,384]{3,2,1,0:T(2,128)} %bitcast.5, ...), custom_call_target="tpu_custom_call" | custom-call | tf_op jit(solution)/shard_map/stage/pallas_call | solution.py:412
  2.0 0.7 %collective-permute-start.1 = (bf16[3,128,384]{2,1,0:T(8,128)(2,1)S(1)}, bf16[3,128,384]{2,1,0:T(8,128)(2,1)S(1)}, u32[]{:S(2)}, u32[]{:S(2)}) collective-permute-start(bf16[3,128,384]{2,1,0:T(8,128)(2,1)S(1)} %get-tuple-element.34), channel_id=1, source_target_pairs={{0,1},{1,0},{2,3},{3,2},{4,5},{5,4},{6,7},{7,6},{8,9},{9,8},{10,11... | collective-permute-start | bytes 884744 | tf_op jit(solution)/shard_map/ppermute | solution.py:482
  2.8 3.0 %collective-permute-start = (bf16[3,128,384]{2,1,0:T(8,128)(2,1)S(1)}, bf16[3,128,384]{2,1,0:T(8,128)(2,1)S(1)}, u32[]{:S(2)}, u32[]{:S(2)}) collective-permute-start(bf16[3,128,384]{2,1,0:T(8,128)(2,1)S(1)} %get-tuple-element.32), channel_id=1, source_target_pairs={{1,2},{3,4},{5,6},{7,8},{9,10},{11,12},{13,14},{2,1},{4,3},{6,5},{... | collective-permute-start | bytes 884744 | tf_op jit(solution)/shard_map/ppermute | solution.py:481
  5.8 3.7 %shard_map.131 = (f32[8,128,384]{2,1,0:T(8,128)S(1)}, bf16[384,1536]{1,0:T(8,128)(2,1)S(1)}, bf16[384,1536]{1,0:T(8,128)(2,1)S(1)}, bf16[384,256]{1,0:T(8,128)(2,1)S(1)}) custom-call(bf16[8,128,384]{2,1,0:T(8,128)(2,1)S(1)} %get-tuple-element.25.refs_0_, f32[7,7,2,384]{3,2,1,0:T(2,128)S(1)} %get-tuple-element.26.refs_1_.refs_4_, ...), custom_call_target="tpu_custom_call" | custom-call | flops 23592960 | bytes 3145728 | tf_op jit(solution)/shard_map/pallas_call | solution.py:344
  9.6 0.0 collective-permute-done.1.refs_7_
  9.6 4.0 %shard_map.132 = (bf16[5,128,384]{2,1,0:T(8,128)(2,1)S(1)}, bf16[16,5,8,256]{3,2,1,0:T(8,128)(2,1)S(1)}) custom-call(bf16[8,128,384]{2,1,0:T(8,128)(2,1)S(1)} %get-tuple-element.25.refs_0_, f32[8,128,384]{2,1,0:T(8,128)S(1)} %get-tuple-element.27.refs_1_, bf16[384,1536]{1,0:T(8,128)(2,1)S(1)} %get-tuple-element.28.refs_2_, ...), custom_call_target="tpu_custom_call" | custom-call | flops 1509949440 | bytes 3440640 | tf_op jit(solution)/shard_map/pallas_call | solution.py:373
  13.6 0.4 collective-permute-done.refs_7_
  14.0 0.0 copy-start
  14.0 0.0 copy-start.1
  14.0 3.3 %shard_map.133 = (bf16[8,128,384]{2,1,0:T(8,128)(2,1)S(1)}, bf16[16,8,8,256]{3,2,1,0:T(8,128)(2,1)S(1)}, bf16[8,128,384]{2,1,0:T(8,128)(2,1)S(1)}, s32[8,128]{1,0:T(8,128)S(1)}, bf16[256,384]{1,0:T(8,128)(2,1)S(1)}) custom-call(bf16[8,128,384]{2,1,0:T(8,128)(2,1)S(1)} %get-tuple-element.25.refs_0_, f32[8,128,384]{2,1,0:T(8,128)S(1)} %get-tuple-element.27.refs_1_, ...), custom_call_target="tpu_custom_call" | custom-call | flops 905969664 | bytes 2064384 | tf_op jit(solution)/shard_map/pallas_call | solution.py:373
  17.3 19.0 %all_to_all.10.x_ref = bf16[16,8,8,256]{3,2,1,0:T(8,128)(2,1)S(1)} all-to-all(bf16[16,8,8,256]{3,2,1,0:T(8,128)(2,1)S(1)} %get-tuple-element.38), channel_id=1, replica_groups=mesh['ens'=2,'band'=16] {'band'}, dimensions={0} | all-to-all | bytes 1048576 | tf_op jit(solution)/shard_map/all_to_all | solution.py:513
  36.2 0.0 copy-done
  36.2 0.0 copy-done.1
  36.2 0.7 %pick.1 = bf16[16,8,8,256]{3,2,1,0:T(8,128)(2,1)S(1)} custom-call(s32[16]{0:T(128)S(1)} %copy-done, s32[128]{0:T(128)S(1)} %copy-done.1, bf16[16,8,8,256]{3,2,1,0:T(8,128)(2,1)S(1)} %all_to_all.10.x_ref), custom_call_target="tpu_custom_call" | custom-call | tf_op jit(solution)/shard_map/pick/pallas_call | solution.py:436
  37.0 18.2 %all_to_all.11.moved_ref = bf16[16,8,8,256]{3,2,1,0:T(8,128)(2,1)S(1)} all-to-all(bf16[16,8,8,256]{3,2,1,0:T(8,128)(2,1)S(1)} %pick.1), channel_id=1, replica_groups=mesh['ens'=2,'band'=16] {'band'}, dimensions={0} | all-to-all | bytes 1048576 | tf_op jit(solution)/shard_map/all_to_all | solution.py:515
  55.2 0.5 ocean_in.1
  55.7 0.1 slice_bitcast_fusion
  55.8 0.1 collective-permute-start.3
  55.9 3.1 %collective-permute-start.2 = (bf16[3,128,384]{2,1,0:T(8,128)(2,1)S(1)}, bf16[3,128,384]{2,1,0:T(8,128)(2,1)S(1)}, u32[]{:S(2)}, u32[]{:S(2)}) collective-permute-start(bf16[3,128,384]{2,1,0:T(8,128)(2,1)S(1)} %get-tuple-element.49), channel_id=1, source_target_pairs={{1,2},{3,4},{5,6},{7,8},{9,10},{11,12},{13,14},{2,1},{4,3},{6,5},{... | collective-permute-start | bytes 884744 | tf_op jit(solution)/shard_map/ppermute | solution.py:481
  59.0 3.7 %shard_map.134 = (f32[8,128,384]{2,1,0:T(8,128)S(1)}, bf16[384,1536]{1,0:T(8,128)(2,1)S(1)}, bf16[384,1536]{1,0:T(8,128)(2,1)S(1)}, bf16[8,128,384]{2,1,0:T(8,128)(2,1)}) custom-call(bf16[8,128,384]{2,1,0:T(8,128)(2,1)S(1)} %get-tuple-element.41.refs_0_, f32[7,7,2,384]{3,2,1,0:T(2,128)S(1)} %get-tuple-element.26.refs_1_.refs_4_, ...), custom_call_target="tpu_custom_call" | custom-call | flops 23592960 | bytes 3145728 | tf_op jit(solution)/shard_map/pallas_call | solution.py:344
  62.7 0.0 collective-permute-done.3.refs_7_
  62.7 3.7 %shard_map.135.refs_8_ = bf16[5,128,384]{2,1,0:T(8,128)(2,1)S(1)} custom-call(bf16[8,128,384]{2,1,0:T(8,128)(2,1)S(1)} %get-tuple-element.41.refs_0_, f32[8,128,384]{2,1,0:T(8,128)S(1)} %get-tuple-element.44.refs_1_, bf16[384,1536]{1,0:T(8,128)(2,1)S(1)} %get-tuple-element.45.refs_2_, bf16[384,1536]{1,0:T(8,128)(2,1)S(1)} %get-tuple-element.46.refs_3_, ...), custom_call_target="tpu_custom_call" | custom-call | flops 1509949440 | bytes 3440640 | tf_op jit(solution)/shard_map/pallas_call | solution.py:373
  66.4 0.7 collective-permute-done.2.refs_7_
  67.1 3.4 %shard_map.136 = bf16[8,128,384]{2,1,0:T(8,128)(2,1)} custom-call(bf16[8,128,384]{2,1,0:T(8,128)(2,1)S(1)} %get-tuple-element.41.refs_0_, f32[8,128,384]{2,1,0:T(8,128)S(1)} %get-tuple-element.44.refs_1_, bf16[384,1536]{1,0:T(8,128)(2,1)S(1)} %get-tuple-element.45.refs_2_, bf16[384,1536]{1,0:T(8,128)(2,1)S(1)} %get-tuple-element.46.refs_3_, ...), custom_call_target="tpu_custom_call" | custom-call | flops 905969664 | bytes 2064384 | tf_op jit(solution)/shard_map/pallas_call | solution.py:373
Async XLA Ops:
  2.0 7.5 %collective-permute-start.1 = (bf16[3,128,384]{2,1,0:T(8,128)(2,1)S(1)}, bf16[3,128,384]{2,1,0:T(8,128)(2,1)S(1)}, u32[]{:S(2)}, u32[]{:S(2)}) collective-permute-start(bf16[3,128,384]{2,1,0:T(8,128)(2,1)S(1)} %get-tuple-element.34), channel_id=1, source_target_pairs={{0,1},{1,0},{2,3},{3,2},{4,5},{5,4},{6,7},{7,6},{8,9},{9,8},{10,11... | collective-permute-start | bytes 884744 | tf_op jit(solution)/shard_map/ppermute | solution.py:482
  2.8 11.2 %collective-permute-start = (bf16[3,128,384]{2,1,0:T(8,128)(2,1)S(1)}, bf16[3,128,384]{2,1,0:T(8,128)(2,1)S(1)}, u32[]{:S(2)}, u32[]{:S(2)}) collective-permute-start(bf16[3,128,384]{2,1,0:T(8,128)(2,1)S(1)} %get-tuple-element.32), channel_id=1, source_target_pairs={{1,2},{3,4},{5,6},{7,8},{9,10},{11,12},{13,14},{2,1},{4,3},{6,5},{... | collective-permute-start | bytes 884744 | tf_op jit(solution)/shard_map/ppermute | solution.py:481
  14.0 22.3 %copy-start = (s32[16]{0:T(128)S(1)}, s32[16]{0:T(128)}, u32[]{:S(2)}) copy-start(s32[16]{0:T(128)} %partner_ref.1) | copy-start | bytes 196
  14.0 22.3 %copy-start.1 = (s32[128]{0:T(128)S(1)}, s32[128]{0:T(128)}, u32[]{:S(2)}) copy-start(s32[128]{0:T(128)} %remap_ref.1) | copy-start | bytes 1540
  55.8 6.9 %collective-permute-start.3 = (bf16[3,128,384]{2,1,0:T(8,128)(2,1)S(1)}, bf16[3,128,384]{2,1,0:T(8,128)(2,1)S(1)}, u32[]{:S(2)}, u32[]{:S(2)}) collective-permute-start(bf16[3,128,384]{2,1,0:T(8,128)(2,1)S(1)} %get-tuple-element.48), channel_id=1, source_target_pairs={{0,1},{1,0},{2,3},{3,2},{4,5},{5,4},{6,7},{7,6},{8,9},{9,8},{10,11... | collective-permute-start | bytes 884744 | tf_op jit(solution)/shard_map/ppermute | solution.py:482
  55.9 11.2 %collective-permute-start.2 = (bf16[3,128,384]{2,1,0:T(8,128)(2,1)S(1)}, bf16[3,128,384]{2,1,0:T(8,128)(2,1)S(1)}, u32[]{:S(2)}, u32[]{:S(2)}) collective-permute-start(bf16[3,128,384]{2,1,0:T(8,128)(2,1)S(1)} %get-tuple-element.49), channel_id=1, source_target_pairs={{1,2},{3,4},{5,6},{7,8},{9,10},{11,12},{13,14},{2,1},{4,3},{6,5},{... | collective-permute-start | bytes 884744 | tf_op jit(solution)/shard_map/ppermute | solution.py:481

commit v4 on v3

--- a/solution.py
+++ b/solution.py
@@ -193,15 +193,31 @@
     ]
     for copy in copies:
         copy.start()
-    fill(lambda m, lons, lanes: x_ref[m, lons, lanes], own_rows(plan), derived, width, lane_blocks)
     tap_rows(kernel, which, plan, weights)
     wide = 2 if width % (2 * SUB) == 0 else 1
+    size = wide * SUB
+    combine = own_rows(plan)
+
+    def prepare(cb, start):
+        lanes = slice(cb * LANES, (cb + 1) * LANES)
+        values = combine(lambda m: x_ref[m, pl.ds(start, size), lanes].astype(F32))
+        for n, value in enumerate(values):
+            derived[cb, n, pl.ds(start + SUB, size), :] = value
+
+    def wrap(cb):
+        for n in range(len(plan.leaves)):
+            derived[cb, n, 0:SUB, :] = derived[cb, n, width : width + SUB, :]
+            derived[cb, n, width + SUB : width + 2 * SUB, :] = derived[cb, n, SUB : 2 * SUB, :]
+
+    for start in range(0, width, size):
+        prepare(0, start)
     for cb in range(lane_blocks):
         lanes = slice(cb * LANES, (cb + 1) * LANES)
-
-        @pl.loop(0, width // (wide * SUB))
+        wrap(cb)
+
+        @pl.loop(0, width // size)
         def _(step):
-            start = pl.multiple_of(step * (wide * SUB), wide * SUB)
+            start = pl.multiple_of(step * size, size)
             done = {}
 
             def value(node):
@@ -216,6 +232,8 @@
             for i, node in enumerate(plan.outs):
                 for v, part in enumerate(value(node)):
                     acc_ref[i, pl.ds(start + v * SUB, SUB), lanes] = part
+            if cb + 1 < lane_blocks:
+                prepare(cb + 1, start)
 
     for copy in copies:
         copy.wait()
@@ -423,8 +441,10 @@
 def pick_kernel(partner_ref, remap_ref, x_ref, out_ref):
     bands, rows = out_ref.shape[:2]
     for o in range(bands):
+        band = partner_ref[o]
+        picked = [x_ref[band, remap_ref[o * rows + r]] for r in range(rows)]
         for r in range(rows):
-            out_ref[o, r] = x_ref[partner_ref[o], remap_ref[o * rows + r]]
+            out_ref[o, r] = picked[r]
 
 
 def pick_rows(x, partner, remap):

time: 71.2 us -> 71.1 us (level)
  no operation moved by 1% of the time
where the time goes in v4:
time: 71.1 us; the launch traced here: 70.7 us
  blocking collectives  37.2 us (52%)
  Pallas kernels  24.2 us (34%)
  starting transfers between devices  6.95 us (10%)
  waiting for transfers between devices  1.35 us (2%)
  between operations  0.91 us (1%)
    all_to_all x1, blocking collectives, per_device(): lax.all_to_all(surface, 'band', split_axis=0, concat_axis=0, tiled=True)  19 us
    all_to_all x1, blocking collectives, per_device(): lax.all_to_all(picked, 'band', split_axis=0, concat_axis=0, tiled=True)  18.2 us
    pallas_call x4, Pallas kernels, side(): pl.pallas_call(functools.partial(side_kernel, (which, has_flux, split, fi...  14.3 us
    pallas_call x2, Pallas kernels, mix(): pl.pallas_call(functools.partial(own_kernel, which), out_shape=[pltpu.VME...  7.21 us
    ppermute x2, starting transfers between devices, halos(): two = lax.ppermute(two, 'band', outer)  6.14 us
  transfers between devices with their start and end apart: 4, of which 2 were waited for; matrix products, arithmetic and copies ran while one was open for 0% of the time, Pallas kernels for 21%

profile of v4, /device:TPU:9, one launch (start us, length us, event | category | flops | bytes accessed | tf_op | source)
XLA Modules:
  0.0 70.7 jit_solution(6306810225865471329)
XLA Ops:
  0.6 1.4 %stage.1 = (bf16[8,128,384]{2,1,0:T(8,128)(2,1)S(1)}, bf16[3,128,384]{2,1,0:T(8,128)(2,1)S(1)}, bf16[3,128,384]{2,1,0:T(8,128)(2,1)S(1)}, f32[7,7,2,384]{3,2,1,0...) custom-call(bf16[8,128,384]{2,1,0:T(8,128)(2,1)} %x_hbm.1, f32[7,7,2,384]{3,2,1,0:T(2,128)} %bitcast.5, ...), custom_call_target="tpu_custom_call" | custom-call | tf_op jit(solution)/shard_map/stage/pallas_call | solution.py:430
  2.0 0.7 %collective-permute-start.1 = (bf16[3,128,384]{2,1,0:T(8,128)(2,1)S(1)}, bf16[3,128,384]{2,1,0:T(8,128)(2,1)S(1)}, u32[]{:S(2)}, u32[]{:S(2)}) collective-permute-start(bf16[3,128,384]{2,1,0:T(8,128)(2,1)S(1)} %get-tuple-element.34), channel_id=1, source_target_pairs={{0,1},{1,0},{2,3},{3,2},{4,5},{5,4},{6,7},{7,6},{8,9},{9,8},{10,11... | collective-permute-start | bytes 884744 | tf_op jit(solution)/shard_map/ppermute | solution.py:502
  2.8 3.0 %collective-permute-start = (bf16[3,128,384]{2,1,0:T(8,128)(2,1)S(1)}, bf16[3,128,384]{2,1,0:T(8,128)(2,1)S(1)}, u32[]{:S(2)}, u32[]{:S(2)}) collective-permute-start(bf16[3,128,384]{2,1,0:T(8,128)(2,1)S(1)} %get-tuple-element.32), channel_id=1, source_target_pairs={{1,2},{3,4},{5,6},{7,8},{9,10},{11,12},{13,14},{2,1},{4,3},{6,5},{... | collective-permute-start | bytes 884744 | tf_op jit(solution)/shard_map/ppermute | solution.py:501
  5.8 3.6 %shard_map.131 = (f32[8,128,384]{2,1,0:T(8,128)S(1)}, bf16[384,1536]{1,0:T(8,128)(2,1)S(1)}, bf16[384,1536]{1,0:T(8,128)(2,1)S(1)}, bf16[384,256]{1,0:T(8,128)(2,1)S(1)}) custom-call(bf16[8,128,384]{2,1,0:T(8,128)(2,1)S(1)} %get-tuple-element.25.refs_0_, f32[7,7,2,384]{3,2,1,0:T(2,128)S(1)} %get-tuple-element.26.refs_1_.refs_4_, ...), custom_call_target="tpu_custom_call" | custom-call | flops 23592960 | bytes 3145728 | tf_op jit(solution)/shard_map/pallas_call | solution.py:362
  9.4 0.0 collective-permute-done.1.refs_7_
  9.5 4.0 %shard_map.132 = (bf16[5,128,384]{2,1,0:T(8,128)(2,1)S(1)}, bf16[16,5,8,256]{3,2,1,0:T(8,128)(2,1)S(1)}) custom-call(bf16[8,128,384]{2,1,0:T(8,128)(2,1)S(1)} %get-tuple-element.25.refs_0_, f32[8,128,384]{2,1,0:T(8,128)S(1)} %get-tuple-element.27.refs_1_, bf16[384,1536]{1,0:T(8,128)(2,1)S(1)} %get-tuple-element.28.refs_2_, ...), custom_call_target="tpu_custom_call" | custom-call | flops 1509949440 | bytes 3440640 | tf_op jit(solution)/shard_map/pallas_call | solution.py:391
  13.4 0.5 collective-permute-done.refs_7_
  14.0 0.0 copy-start
  14.0 0.0 copy-start.1
  14.0 3.3 %shard_map.133 = (bf16[8,128,384]{2,1,0:T(8,128)(2,1)S(1)}, bf16[16,8,8,256]{3,2,1,0:T(8,128)(2,1)S(1)}, bf16[8,128,384]{2,1,0:T(8,128)(2,1)S(1)}, s32[8,128]{1,0:T(8,128)S(1)}, bf16[256,384]{1,0:T(8,128)(2,1)S(1)}) custom-call(bf16[8,128,384]{2,1,0:T(8,128)(2,1)S(1)} %get-tuple-element.25.refs_0_, f32[8,128,384]{2,1,0:T(8,128)S(1)} %get-tuple-element.27.refs_1_, ...), custom_call_target="tpu_custom_call" | custom-call | flops 905969664 | bytes 2064384 | tf_op jit(solution)/shard_map/pallas_call | solution.py:391
  17.3 19.0 %all_to_all.10.x_ref = bf16[16,8,8,256]{3,2,1,0:T(8,128)(2,1)S(1)} all-to-all(bf16[16,8,8,256]{3,2,1,0:T(8,128)(2,1)S(1)} %get-tuple-element.38), channel_id=1, replica_groups=mesh['ens'=2,'band'=16] {'band'}, dimensions={0} | all-to-all | bytes 1048576 | tf_op jit(solution)/shard_map/all_to_all | solution.py:533
  36.2 0.0 copy-done
  36.2 0.0 copy-done.1
  36.2 0.7 %pick.1 = bf16[16,8,8,256]{3,2,1,0:T(8,128)(2,1)S(1)} custom-call(s32[16]{0:T(128)S(1)} %copy-done, s32[128]{0:T(128)S(1)} %copy-done.1, bf16[16,8,8,256]{3,2,1,0:T(8,128)(2,1)S(1)} %all_to_all.10.x_ref), custom_call_target="tpu_custom_call" | custom-call | tf_op jit(solution)/shard_map/pick/pallas_call | solution.py:456
  37.0 18.2 %all_to_all.11.moved_ref = bf16[16,8,8,256]{3,2,1,0:T(8,128)(2,1)S(1)} all-to-all(bf16[16,8,8,256]{3,2,1,0:T(8,128)(2,1)S(1)} %pick.1), channel_id=1, replica_groups=mesh['ens'=2,'band'=16] {'band'}, dimensions={0} | all-to-all | bytes 1048576 | tf_op jit(solution)/shard_map/all_to_all | solution.py:535
  55.2 0.5 ocean_in.1
  55.7 0.1 slice_bitcast_fusion
  55.8 0.1 collective-permute-start.3
  55.9 3.1 %collective-permute-start.2 = (bf16[3,128,384]{2,1,0:T(8,128)(2,1)S(1)}, bf16[3,128,384]{2,1,0:T(8,128)(2,1)S(1)}, u32[]{:S(2)}, u32[]{:S(2)}) collective-permute-start(bf16[3,128,384]{2,1,0:T(8,128)(2,1)S(1)} %get-tuple-element.49), channel_id=1, source_target_pairs={{1,2},{3,4},{5,6},{7,8},{9,10},{11,12},{13,14},{2,1},{4,3},{6,5},{... | collective-permute-start | bytes 884744 | tf_op jit(solution)/shard_map/ppermute | solution.py:501
  59.0 3.6 %shard_map.134 = (f32[8,128,384]{2,1,0:T(8,128)S(1)}, bf16[384,1536]{1,0:T(8,128)(2,1)S(1)}, bf16[384,1536]{1,0:T(8,128)(2,1)S(1)}, bf16[8,128,384]{2,1,0:T(8,128)(2,1)}) custom-call(bf16[8,128,384]{2,1,0:T(8,128)(2,1)S(1)} %get-tuple-element.41.refs_0_, f32[7,7,2,384]{3,2,1,0:T(2,128)S(1)} %get-tuple-element.26.refs_1_.refs_4_, ...), custom_call_target="tpu_custom_call" | custom-call | flops 23592960 | bytes 3145728 | tf_op jit(solution)/shard_map/pallas_call | solution.py:362
  62.6 0.0 collective-permute-done.3.refs_7_
  62.6 3.6 %shard_map.135.refs_8_ = bf16[5,128,384]{2,1,0:T(8,128)(2,1)S(1)} custom-call(bf16[8,128,384]{2,1,0:T(8,128)(2,1)S(1)} %get-tuple-element.41.refs_0_, f32[8,128,384]{2,1,0:T(8,128)S(1)} %get-tuple-element.44.refs_1_, bf16[384,1536]{1,0:T(8,128)(2,1)S(1)} %get-tuple-element.45.refs_2_, bf16[384,1536]{1,0:T(8,128)(2,1)S(1)} %get-tuple-element.46.refs_3_, ...), custom_call_target="tpu_custom_call" | custom-call | flops 1509949440 | bytes 3440640 | tf_op jit(solution)/shard_map/pallas_call | solution.py:391
  66.3 0.8 %collective-permute-done.2.refs_7_ = bf16[3,128,384]{2,1,0:T(8,128)(2,1)S(1)} collective-permute-done((bf16[3,128,384]{2,1,0:T(8,128)(2,1)S(1)}, bf16[3,128,384]{2,1,0:T(8,128)(2,1)S(1)}, u32[]{:S(2)}, u32[]{:S(2)}) %collective-permute-start.2) | collective-permute-done | bytes 294944 | tf_op jit(solution)/shard_map/ppermute | solution.py:501
  67.1 3.4 %shard_map.136 = bf16[8,128,384]{2,1,0:T(8,128)(2,1)} custom-call(bf16[8,128,384]{2,1,0:T(8,128)(2,1)S(1)} %get-tuple-element.41.refs_0_, f32[8,128,384]{2,1,0:T(8,128)S(1)} %get-tuple-element.44.refs_1_, bf16[384,1536]{1,0:T(8,128)(2,1)S(1)} %get-tuple-element.45.refs_2_, bf16[384,1536]{1,0:T(8,128)(2,1)S(1)} %get-tuple-element.46.refs_3_, ...), custom_call_target="tpu_custom_call" | custom-call | flops 905969664 | bytes 2064384 | tf_op jit(solution)/shard_map/pallas_call | solution.py:391
Async XLA Ops:
  2.0 7.4 %collective-permute-start.1 = (bf16[3,128,384]{2,1,0:T(8,128)(2,1)S(1)}, bf16[3,128,384]{2,1,0:T(8,128)(2,1)S(1)}, u32[]{:S(2)}, u32[]{:S(2)}) collective-permute-start(bf16[3,128,384]{2,1,0:T(8,128)(2,1)S(1)} %get-tuple-element.34), channel_id=1, source_target_pairs={{0,1},{1,0},{2,3},{3,2},{4,5},{5,4},{6,7},{7,6},{8,9},{9,8},{10,11... | collective-permute-start | bytes 884744 | tf_op jit(solution)/shard_map/ppermute | solution.py:502
  2.8 11.2 %collective-permute-start = (bf16[3,128,384]{2,1,0:T(8,128)(2,1)S(1)}, bf16[3,128,384]{2,1,0:T(8,128)(2,1)S(1)}, u32[]{:S(2)}, u32[]{:S(2)}) collective-permute-start(bf16[3,128,384]{2,1,0:T(8,128)(2,1)S(1)} %get-tuple-element.32), channel_id=1, source_target_pairs={{1,2},{3,4},{5,6},{7,8},{9,10},{11,12},{13,14},{2,1},{4,3},{6,5},{... | collective-permute-start | bytes 884744 | tf_op jit(solution)/shard_map/ppermute | solution.py:501
  14.0 22.3 %copy-start = (s32[16]{0:T(128)S(1)}, s32[16]{0:T(128)}, u32[]{:S(2)}) copy-start(s32[16]{0:T(128)} %partner_ref.1) | copy-start | bytes 196
  14.0 22.3 %copy-start.1 = (s32[128]{0:T(128)S(1)}, s32[128]{0:T(128)}, u32[]{:S(2)}) copy-start(s32[128]{0:T(128)} %remap_ref.1) | copy-start | bytes 1540
  55.8 6.8 %collective-permute-start.3 = (bf16[3,128,384]{2,1,0:T(8,128)(2,1)S(1)}, bf16[3,128,384]{2,1,0:T(8,128)(2,1)S(1)}, u32[]{:S(2)}, u32[]{:S(2)}) collective-permute-start(bf16[3,128,384]{2,1,0:T(8,128)(2,1)S(1)} %get-tuple-element.48), channel_id=1, source_target_pairs={{0,1},{1,0},{2,3},{3,2},{4,5},{5,4},{6,7},{7,6},{8,9},{9,8},{10,11... | collective-permute-start | bytes 884744 | tf_op jit(solution)/shard_map/ppermute | solution.py:502
  55.9 11.2 %collective-permute-start.2 = (bf16[3,128,384]{2,1,0:T(8,128)(2,1)S(1)}, bf16[3,128,384]{2,1,0:T(8,128)(2,1)S(1)}, u32[]{:S(2)}, u32[]{:S(2)}) collective-permute-start(bf16[3,128,384]{2,1,0:T(8,128)(2,1)S(1)} %get-tuple-element.49), channel_id=1, source_target_pairs={{1,2},{3,4},{5,6},{7,8},{9,10},{11,12},{13,14},{2,1},{4,3},{6,5},{... | collective-permute-start | bytes 884744 | tf_op jit(solution)/shard_map/ppermute | solution.py:501

commit v5 on v4

--- a/solution.py
+++ b/solution.py
@@ -144,26 +144,41 @@
     return half + half * jnp.tanh(u * (0.7978845608028654 + 0.035677408136300125 * (u * u)))
 
 
-def expand(which, total, gain, wu, bu, hidden):
+def expand(which, total, gain, wu, bu, hidden, beside=()):
+    beside = list(beside)
+    tiles = hidden.shape[1] // TILE
+    each = -(-len(beside) // tiles)
     center = jnp.mean(total, axis=-1, keepdims=True)
     total = total - center
     spread = jnp.mean(total * total, axis=-1, keepdims=True)
     normed = (total * lax.rsqrt(spread + 1e-6) * gain[which : which + 1, :]).astype(BF16)
-    for n in range(hidden.shape[1] // TILE):
+    for n in range(tiles):
         cols = slice(n * TILE, (n + 1) * TILE)
         u = jnp.dot(normed, wu[:, cols], preferred_element_type=F32)
         hidden[:, cols] = gelu(u + bu[which : which + 1, cols]).astype(BF16)
-
-
-def contract(split, base, hidden, x_ref, wd, out, begin, size, flux_refs):
+        for step in beside[n * each : (n + 1) * each]:
+            step()
+
+
+def contract(split, base, hidden, x_ref, wd, out, flux_refs, beside=(), ready=None):
     count, width, channels = out.shape
-    cols = slice(begin, begin + size)
-    update = lax.dot_general(
-        hidden[...], wd[cols, :], (((1,), (1,)), ((), ())), preferred_element_type=F32
-    )
-    for n in range(count):
-        state = x_ref[base + n, :, cols].astype(F32)
-        out[n, :, cols] = (state + update[n * width : (n + 1) * width]).astype(BF16)
+    beside = list(beside)
+    parts = -(-channels // TILE)
+    each = -(-len(beside) // parts)
+    for part in range(parts):
+        begin = part * TILE
+        size = min(TILE, channels - begin)
+        cols = slice(begin, begin + size)
+        update = lax.dot_general(
+            hidden[...], wd[cols, :], (((1,), (1,)), ((), ())), preferred_element_type=F32
+        )
+        for step in beside[part * each : (part + 1) * each]:
+            step()
+        for n in range(count):
+            state = x_ref[base + n, :, cols].astype(F32)
+            out[n, :, cols] = (state + update[n * width : (n + 1) * width]).astype(BF16)
+        if ready is not None:
+            ready(begin, size)
     if flux_refs:
         fo, surf = flux_refs
         flux = jnp.dot(out[...].reshape(count * width, channels), fo[...], preferred_element_type=F32).astype(BF16)
@@ -239,42 +254,9 @@
         copy.wait()
 
 
-def side_kernel(cfg, *refs):
-    which, has_flux, split, first, prefetch = cfg
-    refs = list(refs)
-    x_ref, acc_ref, wu, wd, kernel, gain, bu, halo_ref = [refs.pop(0) for _ in range(8)]
-    fo = refs.pop(0) if has_flux else None
-    rows, width, channels = x_ref.shape
-    middle = rows - 2 * PAD
-    held = [refs.pop(0) for _ in range((1 + has_flux) * (not first))]
-    sources = [refs.pop(0) for _ in range(prefetch)]
-    surf = None
-    if first:
-        out = refs.pop(0)
-        surf = refs.pop(0) if has_flux else None
-        targets = [refs.pop(0) for _ in range(prefetch)]
-        derived, weights, conv, hidden, sem = refs
-    else:
-        out_all = refs.pop(0)
-        surf_all = refs.pop(0) if has_flux else None
-        targets = [refs.pop(0) for _ in range(prefetch)]
-        derived, weights, conv, hidden, sem, out = refs if not has_flux else (*refs, None)
+def halo_steps(which, before, acc_ref, halo_ref, kernel, derived, weights, conv):
+    rows, width, channels = acc_ref.shape
     lane_blocks = channels // LANES
-    before = parity() if first else 1 - parity()
-    count = PAD + middle if first else PAD
-    base = (1 - before) * (rows - count)
-
-    copies = [(source, target) for source, target in zip(sources, targets)]
-    if not first:
-        place = before * PAD
-        copies.append((held[0], out_all.at[pl.ds(place, PAD + middle)]))
-        if has_flux:
-            out = out_all.at[pl.ds(base, PAD)]
-            copies.append((held[1], surface_rows(split, surf_all, place, PAD + middle)))
-            surf = surface_rows(split, surf_all, base, PAD)
-    copies = [pltpu.make_async_copy(a, b, sem.at[n]) for n, (a, b) in enumerate(copies)]
-    for copy in copies:
-        copy.start()
 
     def rows_of(load):
         d = [load(before * (PAD - 1 - j) + (1 - before) * j) for j in range(PAD)]
@@ -287,40 +269,86 @@
     for n, (_, add, subtract) in enumerate(EDGE_PRODUCTS):
         weights[n, 0:TAPS, :] = taps(add) if subtract is None else taps(add) - taps(subtract)
     wide = 2 if width % (2 * SUB) == 0 else 1
-    for cb in range(lane_blocks):
+
+    def step(cb, start):
         lanes = slice(cb * LANES, (cb + 1) * LANES)
-
-        @pl.loop(0, width // (wide * SUB))
-        def _(step):
-            start = pl.multiple_of(step * (wide * SUB), wide * SUB)
-            done = {}
-            for j, products in enumerate(EDGE_OUTS):
-                row = before * j + (1 - before) * (rows - 1 - j)
-                total = [acc_ref[row, pl.ds(start + v * SUB, SUB), lanes] for v in range(wide)]
-                for n in products:
-                    if n not in done:
-                        done[n] = fir(derived, weights, cb, EDGE_PRODUCTS[n][0], n, start, wide)
-                    total = [a + b for a, b in zip(total, done[n])]
-                for v in range(wide):
-                    conv[row - base, pl.ds(start + v * SUB, SUB), lanes] = total[v]
-
-    if first:
-        for n in range(middle):
-            conv[before * PAD + n] = acc_ref[PAD + n]
-    expand(which, conv[...].reshape(count * width, channels), gain, wu, bu, hidden)
-    if has_flux or first:
-        contract(split, base, hidden, x_ref, wd, out, 0, channels, (fo, surf) if has_flux else None)
-    else:
-        for begin in range(0, channels, TILE):
-            size = min(TILE, channels - begin)
-            contract(split, base, hidden, x_ref, wd, out, begin, size, None)
+        done = {}
+        for j, products in enumerate(EDGE_OUTS):
+            row = before * j + (1 - before) * (rows - 1 - j)
+            total = [acc_ref[row, start + v * SUB : start + (v + 1) * SUB, lanes] for v in range(wide)]
+            for n in products:
+                if n not in done:
+                    done[n] = fir(derived, weights, cb, EDGE_PRODUCTS[n][0], n, start, wide)
+                total = [a + b for a, b in zip(total, done[n])]
+            for v in range(wide):
+                place = before * j + (1 - before) * (PAD - 1 - j)
+                conv[place, start + v * SUB : start + (v + 1) * SUB, lanes] = total[v]
+
+    return [
+        functools.partial(step, cb, start) for cb in range(lane_blocks) for start in range(0, width, wide * SUB)
+    ]
+
+
+def middle_kernel(which, has_flux, split, *refs):
+    refs = list(refs)
+    x_ref, acc_ref, wu, wd, kernel, gain, bu, halo_ref = [refs.pop(0) for _ in range(8)]
+    fo = refs.pop(0) if has_flux else None
+    hidden, out = refs.pop(0), refs.pop(0)
+    surf = refs.pop(0) if has_flux else None
+    derived, weights, near_hidden, conv = refs
+    rows, width, channels = x_ref.shape
+    count = rows - 2 * PAD
+    steps = halo_steps(which, parity(), acc_ref, halo_ref, kernel, derived, weights, conv)
+    total = acc_ref[PAD : PAD + count].reshape(count * width, channels)
+    expand(which, total, gain, wu, bu, hidden, steps)
+    expand(which, conv[...].reshape(PAD * width, channels), gain, wu, bu, near_hidden)
+    base = (1 - parity()) * (rows - PAD)
+    contract(split, base, near_hidden, x_ref, wd, out, (fo, surf) if has_flux else None)
+
+
+def edges_kernel(which, has_flux, split, prefetch, *refs):
+    refs = list(refs)
+    x_ref, acc_ref, wu, wd, kernel, gain, bu, halo_ref = [refs.pop(0) for _ in range(8)]
+    fo = refs.pop(0) if has_flux else None
+    near_hidden, held = refs.pop(0), refs.pop(0)
+    held_surf = refs.pop(0) if has_flux else None
+    sources = [refs.pop(0) for _ in range(prefetch)]
+    out_all = refs.pop(0)
+    surf_all = refs.pop(0) if has_flux else None
+    targets = [refs.pop(0) for _ in range(prefetch)]
+    derived, weights, conv, hidden, sem = refs[:5]
+    rows, width, channels = x_ref.shape
+    middle = rows - 2 * PAD
+    copies = []
+
+    def start(source, target):
+        copies.append(pltpu.make_async_copy(source, target, sem.at[len(copies)]))
+        copies[-1].start()
+
+    for source, target in zip(sources, targets):
+        start(source, target)
+    odd = parity()
+    start(held, out_all.at[pl.ds((1 - odd) * (rows - PAD), PAD)])
+    if has_flux:
+        start(held_surf, surface_rows(split, surf_all, (1 - odd) * (rows - PAD), PAD))
+    steps = halo_steps(which, 1 - odd, acc_ref, halo_ref, kernel, derived, weights, conv)
+    for side, units in enumerate((near_hidden, hidden)):
+        base = PAD if side == 0 else odd * (rows - PAD)
+        number = middle if side == 0 else PAD
+        beside = steps if side == 0 else ()
+        if side == 1:
+            expand(which, conv[...].reshape(PAD * width, channels), gain, wu, bu, units)
+        if has_flux:
+            out, surf = out_all.at[pl.ds(base, number)], surface_rows(split, surf_all, base, number)
+            contract(split, base, units, x_ref, wd, out, (fo, surf), beside)
+            continue
+        out = refs[5].at[side, pl.ds(0, number)]
+
+        def ready(begin, size, out=out, base=base, number=number):
             cols = pl.ds(begin, size)
-            copies.append(
-                pltpu.make_async_copy(
-                    out.at[:, :, cols], out_all.at[pl.ds(base, PAD), :, cols], sem.at[len(copies)]
-                )
-            )
-            copies[-1].start()
+            start(out.at[:, :, cols], out_all.at[pl.ds(base, number), :, cols])
+
+        contract(split, base, units, x_ref, wd, out, None, beside, ready)
     for copy in copies:
         copy.wait()
 
@@ -376,36 +404,45 @@
     )(near(x), near(kernel), *model)
     flushed = [loaded.pop()] if flush is not None else []
 
-    def side(first, halo_rows, held, out_shape, prefetch):
-        count = PAD + middle if first else PAD
-        close = [x, acc, *loaded[:2], kernel, gain, b_up, halo_rows] + loaded[2:] + held
-        scratch = [
-            pltpu.VMEM((blocks, PAD + 1, width + 2 * SUB, LANES), F32),
-            pltpu.VMEM((len(EDGE_PRODUCTS), SUB, channels), F32),
-            pltpu.VMEM((count, width, channels), F32),
-            pltpu.VMEM((count * width, hidden), BF16),
+    full = pltpu.VMEM if has_flux else jax.ShapeDtypeStruct
+    held_shape = [pltpu.VMEM((middle * width, hidden), BF16), pltpu.VMEM((PAD, width, channels), BF16)]
+    out_shape = [full((rows, width, channels), BF16)]
+    if has_flux:
+        held_shape.append(pltpu.VMEM(piece(PAD), BF16))
+        out_shape.append(pltpu.VMEM(piece(rows), BF16))
+    halo_scratch = [
+        pltpu.VMEM((blocks, PAD + 1, width + 2 * SUB, LANES), F32),
+        pltpu.VMEM((len(EDGE_PRODUCTS), SUB, channels), F32),
+    ]
+    base = [x, acc, *loaded[:2], kernel, gain, b_up]
+    close = base + [one] + loaded[2:]
+    held = pl.pallas_call(
+        functools.partial(middle_kernel, which, has_flux, split),
+        out_shape=held_shape,
+        in_specs=[VMEM] * len(close),
+        out_specs=[VMEM] * len(held_shape),
+        scratch_shapes=halo_scratch
+        + [pltpu.VMEM((PAD * width, hidden), BF16), pltpu.VMEM((PAD, width, channels), F32)],
+        compiler_params=pltpu.CompilerParams(vmem_limit_bytes=LIMIT),
+        cost_estimate=cost(middle),
+    )(*[near(v) for v in close])
+    close = base + [two] + loaded[2:] + list(held)
+    out = pl.pallas_call(
+        functools.partial(edges_kernel, which, has_flux, split, len(prefetch)),
+        out_shape=out_shape + [pltpu.VMEM(v.shape, v.dtype) for v in prefetch],
+        in_specs=[VMEM] * len(close) + [ANY] * len(prefetch),
+        out_specs=[VMEM if has_flux else ANY] + [VMEM] * (len(out_shape) - 1 + len(prefetch)),
+        scratch_shapes=halo_scratch
+        + [
+            pltpu.VMEM((PAD, width, channels), F32),
+            pltpu.VMEM((PAD * width, hidden), BF16),
             pltpu.SemaphoreType.DMA((16,)),
         ]
-        if not first:
-            scratch += [] if has_flux else [pltpu.VMEM((count, width, channels), BF16)]
-        return pl.pallas_call(
-            functools.partial(side_kernel, (which, has_flux, split, first, len(prefetch))),
-            out_shape=out_shape + [pltpu.VMEM(v.shape, v.dtype) for v in prefetch],
-            in_specs=[VMEM] * len(close) + [ANY] * len(prefetch),
-            out_specs=[VMEM if first or has_flux else ANY] + [VMEM] * (len(out_shape) - 1 + len(prefetch)),
-            scratch_shapes=scratch,
-            compiler_params=pltpu.CompilerParams(vmem_limit_bytes=LIMIT),
-            cost_estimate=cost(count),
-        )(*[near(v) for v in close], *[far(v) for v in prefetch])
-
-    held_shape = [pltpu.VMEM((PAD + middle, width, channels), BF16)]
-    full = pltpu.VMEM if has_flux else jax.ShapeDtypeStruct
-    out_shape = [full((rows, width, channels), BF16)]
-    if has_flux:
-        held_shape.append(pltpu.VMEM(piece(PAD + middle), BF16))
-        out_shape.append(pltpu.VMEM(piece(rows), BF16))
-    held = side(True, one, [], held_shape, ())
-    return [*side(False, two, list(held), out_shape, prefetch), *flushed]
+        + ([] if has_flux else [pltpu.VMEM((2, PAD, width, channels), BF16)]),
+        compiler_params=pltpu.CompilerParams(vmem_limit_bytes=LIMIT),
+        cost_estimate=cost(2 * PAD),
+    )(*[near(v) for v in close], *[far(v) for v in prefetch])
+    return [*out, *flushed]
 
 
 def stage_kernel(number, x_hbm, *refs):

time: 71.1 us -> 70.8 us (level)
  Pallas kernels: 24.2 us -> 23 us
  waiting for transfers between devices: 1.35 us -> 2.41 us
    pallas_call x4, Pallas kernels: 14.3 us -> 13.2 us  [the longest x2 6.59 us: mix(): pl.pallas_call(functools.partial(edges_kernel, which, has_flux, split, le...]
    ppermute x2, waiting for transfers between devices: 1.35 us -> 2.41 us  [halos(): two = lax.ppermute(two, 'band', outer)]
  transfers between devices with their start and end apart: 4 -> 4, of which waited for: 2 -> 2; matrix products, arithmetic and copies ran while one was open for 0% -> 0% of each run, Pallas kernels for 21% -> 20%
where the time goes in v5:
time: 70.8 us; the launch traced here: 70.6 us
  blocking collectives  37.2 us (53%)
  Pallas kernels  23 us (32%)
  starting transfers between devices  6.95 us (10%)
  waiting for transfers between devices  2.41 us (3%)
  between operations  0.91 us (1%)
    all_to_all x1, blocking collectives, per_device(): lax.all_to_all(surface, 'band', split_axis=0, concat_axis=0, tiled=True)  19 us
    all_to_all x1, blocking collectives, per_device(): lax.all_to_all(picked, 'band', split_axis=0, concat_axis=0, tiled=True)  18.2 us
    pallas_call x2, Pallas kernels, mix(): pl.pallas_call(functools.partial(own_kernel, which), out_shape=[pltpu.VME...  7.21 us
    pallas_call x2, Pallas kernels, mix(): pl.pallas_call(functools.partial(edges_kernel, which, has_flux, split, le...  6.59 us
    pallas_call x2, Pallas kernels, mix(): pl.pallas_call(functools.partial(middle_kernel, which, has_flux, split),...  6.57 us
    ppermute x2, starting transfers between devices, halos(): two = lax.ppermute(two, 'band', outer)  6.14 us
    ppermute x2, waiting for transfers between devices, halos(): two = lax.ppermute(two, 'band', outer)  2.41 us
  transfers between devices with their start and end apart: 4, of which 2 were waited for; matrix products, arithmetic and copies ran while one was open for 0% of the time, Pallas kernels for 20%

profile of v5, /device:TPU:9, one launch (start us, length us, event | category | flops | bytes accessed | tf_op | source)
XLA Modules:
  0.0 70.6 jit_solution(5260946884033862651)
XLA Ops:
  0.6 1.4 %stage.1 = (bf16[8,128,384]{2,1,0:T(8,128)(2,1)S(1)}, bf16[3,128,384]{2,1,0:T(8,128)(2,1)S(1)}, bf16[3,128,384]{2,1,0:T(8,128)(2,1)S(1)}, f32[7,7,2,384]{3,2,1,0...) custom-call(bf16[8,128,384]{2,1,0:T(8,128)(2,1)} %x_hbm.1, f32[7,7,2,384]{3,2,1,0:T(2,128)} %bitcast.5, ...), custom_call_target="tpu_custom_call" | custom-call | tf_op jit(solution)/shard_map/stage/pallas_call | solution.py:467
  2.0 0.7 %collective-permute-start.1 = (bf16[3,128,384]{2,1,0:T(8,128)(2,1)S(1)}, bf16[3,128,384]{2,1,0:T(8,128)(2,1)S(1)}, u32[]{:S(2)}, u32[]{:S(2)}) collective-permute-start(bf16[3,128,384]{2,1,0:T(8,128)(2,1)S(1)} %get-tuple-element.37), channel_id=1, source_target_pairs={{0,1},{1,0},{2,3},{3,2},{4,5},{5,4},{6,7},{7,6},{8,9},{9,8},{10,11... | collective-permute-start | bytes 884744 | tf_op jit(solution)/shard_map/ppermute | solution.py:539
  2.8 3.0 %collective-permute-start = (bf16[3,128,384]{2,1,0:T(8,128)(2,1)S(1)}, bf16[3,128,384]{2,1,0:T(8,128)(2,1)S(1)}, u32[]{:S(2)}, u32[]{:S(2)}) collective-permute-start(bf16[3,128,384]{2,1,0:T(8,128)(2,1)S(1)} %get-tuple-element.35), channel_id=1, source_target_pairs={{1,2},{3,4},{5,6},{7,8},{9,10},{11,12},{13,14},{2,1},{4,3},{6,5},{... | collective-permute-start | bytes 884744 | tf_op jit(solution)/shard_map/ppermute | solution.py:538
  5.8 3.6 %shard_map.131 = (f32[8,128,384]{2,1,0:T(8,128)S(1)}, bf16[384,1536]{1,0:T(8,128)(2,1)S(1)}, bf16[384,1536]{1,0:T(8,128)(2,1)S(1)}, bf16[384,256]{1,0:T(8,128)(2,1)S(1)}) custom-call(bf16[8,128,384]{2,1,0:T(8,128)(2,1)S(1)} %get-tuple-element.28.refs_0_, f32[7,7,2,384]{3,2,1,0:T(2,128)S(1)} %get-tuple-element.29.refs_1_.refs_4_, ...), custom_call_target="tpu_custom_call" | custom-call | flops 23592960 | bytes 3145728 | tf_op jit(solution)/shard_map/pallas_call | solution.py:390
  9.4 0.0 collective-permute-done.1.refs_7_
  9.5 3.4 %shard_map.132 = (bf16[256,1536]{1,0:T(8,128)(2,1)S(1)}, bf16[3,128,384]{2,1,0:T(8,128)(2,1)S(1)}, bf16[16,3,8,256]{3,2,1,0:T(8,128)(2,1)S(1)}) custom-call(bf16[8,128,384]{2,1,0:T(8,128)(2,1)S(1)} %get-tuple-element.28.refs_0_, f32[8,128,384]{2,1,0:T(8,128)S(1)} %get-tuple-element.30.refs_1_, bf16[384,1536]{1,0:T(8,128)(2,1)S(1)} %get-tuple-element.31.refs_2_, ...), custom_call_target="tpu_custom_call" | custom-call | flops 603979776 | bytes 1376256 | tf_op jit(solution)/shard_map/pallas_call | solution.py:419
  12.8 1.1 %collective-permute-done.refs_7_ = bf16[3,128,384]{2,1,0:T(8,128)(2,1)S(1)} collective-permute-done((bf16[3,128,384]{2,1,0:T(8,128)(2,1)S(1)}, bf16[3,128,384]{2,1,0:T(8,128)(2,1)S(1)}, u32[]{:S(2)}, u32[]{:S(2)}) %collective-permute-start) | collective-permute-done | bytes 294944 | tf_op jit(solution)/shard_map/ppermute | solution.py:538
  14.0 0.0 copy-start
  14.0 0.0 copy-start.1
  14.0 3.2 %shard_map.133 = (bf16[8,128,384]{2,1,0:T(8,128)(2,1)S(1)}, bf16[16,8,8,256]{3,2,1,0:T(8,128)(2,1)S(1)}, bf16[8,128,384]{2,1,0:T(8,128)(2,1)S(1)}, s32[8,128]{1,0:T(8,128)S(1)}, bf16[256,384]{1,0:T(8,128)(2,1)S(1)}) custom-call(bf16[8,128,384]{2,1,0:T(8,128)(2,1)S(1)} %get-tuple-element.28.refs_0_, f32[8,128,384]{2,1,0:T(8,128)S(1)} %get-tuple-element.30.refs_1_, ...), custom_call_target="tpu_custom_call" | custom-call | flops 1811939328 | bytes 4128768 | tf_op jit(solution)/shard_map/pallas_call | solution.py:430
  17.2 19.0 %all_to_all.10.x_ref = bf16[16,8,8,256]{3,2,1,0:T(8,128)(2,1)S(1)} all-to-all(bf16[16,8,8,256]{3,2,1,0:T(8,128)(2,1)S(1)} %get-tuple-element.42), channel_id=1, replica_groups=mesh['ens'=2,'band'=16] {'band'}, dimensions={0} | all-to-all | bytes 1048576 | tf_op jit(solution)/shard_map/all_to_all | solution.py:570
  36.2 0.0 copy-done
  36.2 0.0 copy-done.1
  36.2 0.7 %pick.1 = bf16[16,8,8,256]{3,2,1,0:T(8,128)(2,1)S(1)} custom-call(s32[16]{0:T(128)S(1)} %copy-done, s32[128]{0:T(128)S(1)} %copy-done.1, bf16[16,8,8,256]{3,2,1,0:T(8,128)(2,1)S(1)} %all_to_all.10.x_ref), custom_call_target="tpu_custom_call" | custom-call | tf_op jit(solution)/shard_map/pick/pallas_call | solution.py:493
  36.9 18.2 %all_to_all.11.moved_ref = bf16[16,8,8,256]{3,2,1,0:T(8,128)(2,1)S(1)} all-to-all(bf16[16,8,8,256]{3,2,1,0:T(8,128)(2,1)S(1)} %pick.1), channel_id=1, replica_groups=mesh['ens'=2,'band'=16] {'band'}, dimensions={0} | all-to-all | bytes 1048576 | tf_op jit(solution)/shard_map/all_to_all | solution.py:572
  55.2 0.5 ocean_in.1
  55.7 0.1 slice_bitcast_fusion
  55.8 0.1 collective-permute-start.3
  55.8 3.1 %collective-permute-start.2 = (bf16[3,128,384]{2,1,0:T(8,128)(2,1)S(1)}, bf16[3,128,384]{2,1,0:T(8,128)(2,1)S(1)}, u32[]{:S(2)}, u32[]{:S(2)}) collective-permute-start(bf16[3,128,384]{2,1,0:T(8,128)(2,1)S(1)} %get-tuple-element.55), channel_id=1, source_target_pairs={{1,2},{3,4},{5,6},{7,8},{9,10},{11,12},{13,14},{2,1},{4,3},{6,5},{... | collective-permute-start | bytes 884744 | tf_op jit(solution)/shard_map/ppermute | solution.py:538
  58.9 3.6 %shard_map.134 = (f32[8,128,384]{2,1,0:T(8,128)S(1)}, bf16[384,1536]{1,0:T(8,128)(2,1)S(1)}, bf16[384,1536]{1,0:T(8,128)(2,1)S(1)}, bf16[8,128,384]{2,1,0:T(8,128)(2,1)}) custom-call(bf16[8,128,384]{2,1,0:T(8,128)(2,1)S(1)} %get-tuple-element.45.refs_0_, f32[7,7,2,384]{3,2,1,0:T(2,128)S(1)} %get-tuple-element.29.refs_1_.refs_4_, ...), custom_call_target="tpu_custom_call" | custom-call | flops 23592960 | bytes 3145728 | tf_op jit(solution)/shard_map/pallas_call | solution.py:390
  62.6 0.0 collective-permute-done.3.refs_7_
  62.6 3.2 %shard_map.135 = (bf16[256,1536]{1,0:T(8,128)(2,1)S(1)}, bf16[3,128,384]{2,1,0:T(8,128)(2,1)S(1)}) custom-call(bf16[8,128,384]{2,1,0:T(8,128)(2,1)S(1)} %get-tuple-element.45.refs_0_, f32[8,128,384]{2,1,0:T(8,128)S(1)} %get-tuple-element.48.refs_1_, bf16[384,1536]{1,0:T(8,128)(2,1)S(1)} %get-tuple-element.49.refs_2_, ...), custom_call_target="tpu_custom_call" | custom-call | flops 603979776 | bytes 1376256 | tf_op jit(solution)/shard_map/pallas_call | solution.py:419
  65.8 1.3 %collective-permute-done.2.refs_7_ = bf16[3,128,384]{2,1,0:T(8,128)(2,1)S(1)} collective-permute-done((bf16[3,128,384]{2,1,0:T(8,128)(2,1)S(1)}, bf16[3,128,384]{2,1,0:T(8,128)(2,1)S(1)}, u32[]{:S(2)}, u32[]{:S(2)}) %collective-permute-start.2) | collective-permute-done | bytes 294944 | tf_op jit(solution)/shard_map/ppermute | solution.py:538
  67.0 3.3 %shard_map.136 = bf16[8,128,384]{2,1,0:T(8,128)(2,1)} custom-call(bf16[8,128,384]{2,1,0:T(8,128)(2,1)S(1)} %get-tuple-element.45.refs_0_, f32[8,128,384]{2,1,0:T(8,128)S(1)} %get-tuple-element.48.refs_1_, bf16[384,1536]{1,0:T(8,128)(2,1)S(1)} %get-tuple-element.49.refs_2_, bf16[384,1536]{1,0:T(8,128)(2,1)S(1)} %get-tuple-element.50.refs_3_, ...), custom_call_target="tpu_custom_call" | custom-call | flops 1811939328 | bytes 4128768 | tf_op jit(solution)/shard_map/pallas_call | solution.py:430
Async XLA Ops:
  2.0 7.4 %collective-permute-start.1 = (bf16[3,128,384]{2,1,0:T(8,128)(2,1)S(1)}, bf16[3,128,384]{2,1,0:T(8,128)(2,1)S(1)}, u32[]{:S(2)}, u32[]{:S(2)}) collective-permute-start(bf16[3,128,384]{2,1,0:T(8,128)(2,1)S(1)} %get-tuple-element.37), channel_id=1, source_target_pairs={{0,1},{1,0},{2,3},{3,2},{4,5},{5,4},{6,7},{7,6},{8,9},{9,8},{10,11... | collective-permute-start | bytes 884744 | tf_op jit(solution)/shard_map/ppermute | solution.py:539
  2.8 11.2 %collective-permute-start = (bf16[3,128,384]{2,1,0:T(8,128)(2,1)S(1)}, bf16[3,128,384]{2,1,0:T(8,128)(2,1)S(1)}, u32[]{:S(2)}, u32[]{:S(2)}) collective-permute-start(bf16[3,128,384]{2,1,0:T(8,128)(2,1)S(1)} %get-tuple-element.35), channel_id=1, source_target_pairs={{1,2},{3,4},{5,6},{7,8},{9,10},{11,12},{13,14},{2,1},{4,3},{6,5},{... | collective-permute-start | bytes 884744 | tf_op jit(solution)/shard_map/ppermute | solution.py:538
  14.0 22.2 %copy-start = (s32[16]{0:T(128)S(1)}, s32[16]{0:T(128)}, u32[]{:S(2)}) copy-start(s32[16]{0:T(128)} %partner_ref.1) | copy-start | bytes 196
  14.0 22.2 %copy-start.1 = (s32[128]{0:T(128)S(1)}, s32[128]{0:T(128)}, u32[]{:S(2)}) copy-start(s32[128]{0:T(128)} %remap_ref.1) | copy-start | bytes 1540
  55.8 6.8 %collective-permute-start.3 = (bf16[3,128,384]{2,1,0:T(8,128)(2,1)S(1)}, bf16[3,128,384]{2,1,0:T(8,128)(2,1)S(1)}, u32[]{:S(2)}, u32[]{:S(2)}) collective-permute-start(bf16[3,128,384]{2,1,0:T(8,128)(2,1)S(1)} %get-tuple-element.54), channel_id=1, source_target_pairs={{0,1},{1,0},{2,3},{3,2},{4,5},{5,4},{6,7},{7,6},{8,9},{9,8},{10,11... | collective-permute-start | bytes 884744 | tf_op jit(solution)/shard_map/ppermute | solution.py:539
  55.8 11.2 %collective-permute-start.2 = (bf16[3,128,384]{2,1,0:T(8,128)(2,1)S(1)}, bf16[3,128,384]{2,1,0:T(8,128)(2,1)S(1)}, u32[]{:S(2)}, u32[]{:S(2)}) collective-permute-start(bf16[3,128,384]{2,1,0:T(8,128)(2,1)S(1)} %get-tuple-element.55), channel_id=1, source_target_pairs={{1,2},{3,4},{5,6},{7,8},{9,10},{11,12},{13,14},{2,1},{4,3},{6,5},{... | collective-permute-start | bytes 884744 | tf_op jit(solution)/shard_map/ppermute | solution.py:538
